TPU v7x, 32 devices: a whole 2x2x4 slice. The times are simulated.
32 devices in a mesh: groups: 1, rows: 32 (over z, y, x, core).
Axes of the slice: x: 2, y: 2, z: 4, core: 2. Of those that a mesh axis runs over, the one named last changes fastest.
Arguments:
- tokens: bfloat16 [384, 8192], P(('groups', 'rows')), may hold values from -6 to 6
- gate_weight: bfloat16 [8192, 14336], P('rows'), may hold values from -0.0625 to 0.0625
- up_weight: bfloat16 [8192, 14336], P('rows'), may hold values from -0.0625 to 0.0625
- skew_params: float32 [2, 2, 128, 64, 64], P(None, None, 'rows'), may hold values from -0.3125 to 0.3125
- section_bits: int32 [2, 13], replicated, may hold values from 0 to 12, each once within a row
- upstream: bfloat16 [384, 14336], P('groups', 'rows'), may hold values from -0.3125 to 0.3125
Outputs:
- activation: bfloat16 [384, 14336], P('groups', 'rows')
- skew_grad: float32 [2, 2, 128, 64, 64], P('groups', None, 'rows')
Inputs may be any that keep to these rules, and one draw needn't show every extreme that they name: Each row of section_bits names every one of the 13 bit positions once.
All inputs are finite; a program needn't handle non-finite values.
Results may differ from a plain program's by a relative error of at most 0.0093.
Values may be sent and summed in bfloat16 or wider, within the bound.
A program may use at most 192 MiB of HBM per device.

v0:
```python
import jax
import jax.numpy as jnp
from jax import lax
from jax.sharding import PartitionSpec as P


def cayley(skew_blocks):
    extent = skew_blocks.shape[-1]
    identity = jnp.eye(extent, dtype=jnp.float32)
    generator = skew_blocks - jnp.swapaxes(skew_blocks, -1, -2)
    minus_part = identity - generator
    squared = jnp.einsum(
        "...ij,...jk->...ik", minus_part, minus_part, precision=lax.Precision.HIGHEST
    )
    normal = identity - jnp.einsum(
        "...ij,...jk->...ik", generator, generator, precision=lax.Precision.HIGHEST
    )
    lower_factor = jnp.linalg.cholesky(normal)
    halfway = lax.linalg.triangular_solve(lower_factor, squared, left_side=True, lower=True)
    return lax.linalg.triangular_solve(
        lower_factor, halfway, left_side=True, lower=True, transpose_a=True
    )


def slot_order(section_row, extent):
    positions = jnp.arange(extent, dtype=jnp.int32)
    places = jnp.arange(section_row.shape[0], dtype=jnp.int32)
    digits = jnp.right_shift(positions[:, None], places[None, :]) & 1
    return jnp.sum(jnp.left_shift(digits, section_row[None, :]), axis=1)


def inverse_order(section_row, extent):
    positions = jnp.arange(extent, dtype=jnp.int32)
    places = jnp.arange(section_row.shape[0], dtype=jnp.int32)
    digits = jnp.right_shift(positions[:, None], section_row[None, :]) & 1
    return jnp.sum(jnp.left_shift(digits, places[None, :]), axis=1)


def rotate_columns(columns, rotation, orders, inverses):
    kept_inputs = []
    current = columns
    index = orders[0]
    block_count = rotation.shape[1]
    col_count = columns.shape[1]
    section_total = len(orders)
    for section_at in range(section_total):
        permuted = current[index]
        mixed_rows = jnp.einsum(
            "kji,kic->kjc",
            rotation[section_at],
            permuted.reshape(block_count, -1, col_count),
            preferred_element_type=jnp.float32,
        ).astype(jnp.bfloat16)
        kept_inputs.append(permuted)
        current = mixed_rows.reshape(columns.shape)
        if section_at + 1 < section_total:
            index = inverses[section_at][orders[section_at + 1]]
        else:
            index = inverses[section_at]
    return (current[index], kept_inputs)


def unrotate(grad_top, rotation, orders, inverses):
    block_count = rotation.shape[1]
    col_count = grad_top.shape[1]
    section_total = len(orders)
    slot_grads = [None] * section_total
    current = grad_top
    index = orders[section_total - 1]
    for section_at in reversed(range(section_total)):
        permuted = current[index]
        slot_grads[section_at] = permuted
        if section_at > 0:
            pulled = jnp.einsum(
                "kji,kjc->kic",
                rotation[section_at],
                permuted.reshape(block_count, -1, col_count),
                preferred_element_type=jnp.float32,
            ).astype(jnp.bfloat16)
            current = pulled.reshape(grad_top.shape)
            index = inverses[section_at][orders[section_at - 1]]
    return slot_grads


def block_products(slot_grad, slot_input, block_count):
    col_count = slot_grad.shape[-1]
    return jnp.einsum(
        "kjc,kic->kji",
        slot_grad.reshape(block_count, -1, col_count),
        slot_input.reshape(block_count, -1, col_count),
        preferred_element_type=jnp.float32,
    )


def shards(tokens, gate_weight, up_weight, skew_params, section_bits, upstream):
    extent = skew_params.shape[-1]
    model_width = tokens.shape[1]
    block_count = model_width // extent
    section_count = section_bits.shape[0]
    own_rotation, pullback = jax.vjp(cayley, skew_params)
    rotation = lax.all_gather(own_rotation.astype(jnp.bfloat16), "rows", axis=2, tiled=True)
    orders = [
        slot_order(section_bits[section_at], model_width) for section_at in range(section_count)
    ]
    inverses = [
        inverse_order(section_bits[section_at], model_width) for section_at in range(section_count)
    ]
    all_tokens = lax.all_gather(tokens, "rows", axis=0, tiled=True)
    gate_cols, up_cols = (
        lax.all_to_all(gate_weight, "rows", split_axis=1, concat_axis=0, tiled=True),
        lax.all_to_all(up_weight, "rows", split_axis=1, concat_axis=0, tiled=True),
    )
    rotated_gate, gate_inputs = rotate_columns(gate_cols, rotation[0], orders, inverses)
    rotated_up, up_inputs = rotate_columns(up_cols, rotation[1], orders, inverses)
    gate_pre = jnp.dot(all_tokens, rotated_gate, preferred_element_type=jnp.float32)
    up_pre = jnp.dot(all_tokens, rotated_up, preferred_element_type=jnp.float32)
    sigmoid_val = jax.nn.sigmoid(gate_pre)
    silu_val = gate_pre * sigmoid_val
    activation = (silu_val * up_pre).astype(jnp.bfloat16)
    cotangent = upstream.astype(jnp.float32)
    gate_grad = (cotangent * up_pre * sigmoid_val * (1.0 + gate_pre * (1.0 - sigmoid_val))).astype(
        jnp.bfloat16
    )
    up_grad = (cotangent * silu_val).astype(jnp.bfloat16)
    contract = (((0,), (0,)), ((), ()))
    gate_top = lax.dot_general(
        all_tokens, gate_grad, contract, preferred_element_type=jnp.float32
    ).astype(jnp.bfloat16)
    up_top = lax.dot_general(
        all_tokens, up_grad, contract, preferred_element_type=jnp.float32
    ).astype(jnp.bfloat16)
    gate_slots = unrotate(gate_top, rotation[0], orders, inverses)
    up_slots = unrotate(up_top, rotation[1], orders, inverses)
    gate_terms = jnp.stack(
        [
            block_products(gate_slots[section_at], gate_inputs[section_at], block_count)
            for section_at in range(section_count)
        ]
    )
    up_terms = jnp.stack(
        [
            block_products(up_slots[section_at], up_inputs[section_at], block_count)
            for section_at in range(section_count)
        ]
    )
    own_sums = lax.psum_scatter(
        jnp.stack((gate_terms, up_terms)), "rows", scatter_dimension=2, tiled=True
    )
    skew_grad = pullback(own_sums)[0]
    return (activation, skew_grad)


def solution(mesh):
    placed = (
        P(("groups", "rows"), None),
        P("rows", None),
        P("rows", None),
        P(None, None, "rows", None, None),
        P(),
        P("groups", "rows"),
    )
    return jax.shard_map(
        shards,
        mesh=mesh,
        in_specs=placed,
        out_specs=(P("groups", "rows"), P("groups", None, "rows", None, None)),
        check_vma=False,
    )
```

profile of v0, /device:TPU:0, one launch (start us, length us, event | category | flops | bytes accessed | tf_op | source)
XLA Modules:
  0.0 1387.1 jit_solution(2663491135916769819)
XLA Ops:
  7.2 10.2 copy.86
  17.4 7.4 all-to-all-start
  24.8 0.7 all-gather.6.cloned.1.call-update
  25.5 10.2 copy.88
  35.7 190.3 %all-to-all-done = bf16[256,32,448]{0,2,1:T(8,128)(2,1)} async-done(((bf16[256,32,448]{0,2,1:T(8,128)(2,1)}), bf16[256,32,448]{0,2,1:T(8,128)(2,1)}, u32[]{:S(2)}, u32[]{:S(2)}) %all-to-all-start) | async-done | bytes 7340064 | tf_op jit(solution)/shard_map/all_to_all | solution.py:110
  226.0 3.7 all-to-all-start.1
  231.0 93.8 %custom-call.14 = f32[2,2,4,64,64]{4,3,2,1,0:T(8,128)S(1)} custom-call(f32[2,2,4,64,64]{4,3,2,1,0:T(8,128)S(1)} %fusion.35), custom_call_target="Cholesky" | custom-call | tf_op jit(solution)/shard_map/jvp(jit(cholesky))/cholesky | solution.py:18
  325.1 0.7 iota_compare_fusion.3
  325.7 0.9 select_bitcast_fusion.1
  326.7 78.6 %custom-call.22 = f32[2,2,4,1,64,64]{4,5,3,2,1,0:T(8,128)S(1)} custom-call(f32[2,2,4,1,64,64]{5,4,3,2,1,0:T(8,128)S(1)} %get-tuple-element.9), custom_call_target="InvertDiagBlocksLowerTriangular" | custom-call | tf_op jit(solution)/shard_map/jvp()/triangular_solve/custom-call.0 | solution.py:20
  405.4 0.7 fusion.42
  406.0 1.0 fusion.30
  407.0 0.8 copy-done.6
  407.9 1.5 fusion.66
  409.5 0.6 shift-left_reduce_fusion
  410.2 45.7 %gather_fusion.1 = s32[8192]{0:T(1024)S(1)} fusion(s32[8192]{0:T(1024)S(1)} %get-tuple-element.19, s32[8192]{0:T(1024)S(1)} %broadcast_clamp_fusion.3), kind=kCustom, calls=%fused_computation.1 | custom fusion | bytes 98304 | tf_op jit(solution)/shard_map/gather | solution.py:57
  456.0 45.5 %gather_fusion.8 = s32[8192]{0:T(1024)S(1)} fusion(s32[8192]{0:T(1024)S(1)} %get-tuple-element.4, s32[8192]{0:T(1024)S(1)} %broadcast_clamp_fusion.4), kind=kCustom, calls=%fused_computation.8 | custom fusion | bytes 98304 | tf_op jit(solution)/shard_map/gather | solution.py:81
  502.4 8.8 reshape.296
  511.1 11.0 copy.87
  522.1 38.4 %gather_fusion = bf16[8192,448]{1,0:T(8,128)(2,1)} fusion(bf16[8192,448]{1,0:T(8,128)(2,1)} %bitcast.194, s32[8192]{0:T(1024)S(1)} %broadcast_clamp_fusion.4), kind=kCustom, calls=%fused_computation | custom fusion | bytes 14712832 | tf_op jit(solution)/shard_map/gather | solution.py:47
  560.5 11.0 copy.89
  571.6 38.4 %gather_fusion.4 = bf16[8192,448]{1,0:T(8,128)(2,1)} fusion(bf16[8192,448]{1,0:T(8,128)(2,1)} %bitcast.193, s32[8192]{0:T(1024)S(1)} %broadcast_clamp_fusion.4), kind=kCustom, calls=%fused_computation.4 | custom fusion | bytes 14712832 | tf_op jit(solution)/shard_map/gather | solution.py:47
  609.9 9.6 convolution_convert_fusion.7
  619.5 38.4 %gather_fusion.2 = bf16[8192,448]{1,0:T(8,128)(2,1)} fusion(bf16[8192,448]{1,0:T(8,128)(2,1)} %bitcast.191, s32[8192]{0:T(1024)S(1)} %broadcast_clamp_fusion.2), kind=kCustom, calls=%fused_computation.2 | custom fusion | bytes 14712832 | tf_op jit(solution)/shard_map/gather | solution.py:47
  657.9 9.6 convolution_convert_fusion.5
  667.5 38.6 %gather_fusion.5 = bf16[8192,448]{1,0:T(8,128)(2,1)} fusion(bf16[8192,448]{1,0:T(8,128)(2,1)} %bitcast.188, s32[8192]{0:T(1024)S(1)} %broadcast_clamp_fusion.2), kind=kCustom, calls=%fused_computation.5 | custom fusion | bytes 14712832 | tf_op jit(solution)/shard_map/gather | solution.py:47
  706.1 9.6 convolution_convert_fusion.6
  715.7 38.4 %gather_fusion.3 = bf16[8192,448]{1,0:T(8,128)(2,1)} fusion(bf16[8192,448]{1,0:T(8,128)(2,1)} %bitcast.192, s32[8192]{0:T(1024)S(1)} %broadcast_clamp_fusion.1), kind=kCustom, calls=%fused_computation.3 | custom fusion | bytes 14712832 | tf_op jit(solution)/shard_map/gather | solution.py:60
  754.0 9.6 convolution_convert_fusion.4
  763.6 38.4 %gather_fusion.6 = bf16[8192,448]{1,0:T(8,128)(2,1)} fusion(bf16[8192,448]{1,0:T(8,128)(2,1)} %bitcast.189, s32[8192]{0:T(1024)S(1)} %broadcast_clamp_fusion.1), kind=kCustom, calls=%fused_computation.6 | custom fusion | bytes 14712832 | tf_op jit(solution)/shard_map/gather | solution.py:60
  802.0 9.5 convolution_bitcast_fusion.5
  811.5 8.2 multiply_convert_fusion
  819.7 6.0 fusion.1
  825.8 11.0 copy.94
  836.8 38.5 %gather_fusion.10 = bf16[8192,448]{1,0:T(8,128)(2,1)} fusion(bf16[8192,448]{1,0:T(8,128)(2,1)} %copy.94, s32[8192]{0:T(1024)S(1)} %copy-done.15), kind=kCustom, calls=%fused_computation.10 | custom fusion | bytes 14712832 | tf_op jit(solution)/shard_map/gather | solution.py:71
  875.3 10.1 convolution_bitcast_fusion
  885.5 9.7 convolution_convert_fusion.2
  895.2 38.4 %gather_fusion.11 = bf16[8192,448]{1,0:T(8,128)(2,1)} fusion(bf16[8192,448]{1,0:T(8,128)(2,1)} %bitcast.190, s32[8192]{0:T(1024)S(1)} %copy-done.16), kind=kCustom, calls=%fused_computation.11 | custom fusion | bytes 14712832 | tf_op jit(solution)/shard_map/gather | solution.py:71
  933.5 10.1 convolution_bitcast_fusion.1
  943.6 8.8 fusion
  952.5 11.0 copy.92
  963.5 38.5 %gather_fusion.7 = bf16[8192,448]{1,0:T(8,128)(2,1)} fusion(bf16[8192,448]{1,0:T(8,128)(2,1)} %copy.92, s32[8192]{0:T(1024)S(1)} %copy-done.15), kind=kCustom, calls=%fused_computation.7 | custom fusion | bytes 14712832 | tf_op jit(solution)/shard_map/gather | solution.py:71
  1002.0 10.2 convolution_bitcast_fusion.2
  1012.2 9.7 convolution_convert_fusion.3
  1021.9 38.4 %gather_fusion.9 = bf16[8192,448]{1,0:T(8,128)(2,1)} fusion(bf16[8192,448]{1,0:T(8,128)(2,1)} %bitcast.187, s32[8192]{0:T(1024)S(1)} %copy-done.16), kind=kCustom, calls=%fused_computation.9 | custom fusion | bytes 14712832 | tf_op jit(solution)/shard_map/gather | solution.py:71
  1060.2 10.1 convolution_bitcast_fusion.3
  1070.3 4.6 maximum_bitcast_fusion.1
  1075.0 3.6 maximum_bitcast_fusion
  1078.6 6.2 pad_maximum_fusion
  1084.8 79.7 %custom-call.26 = f32[2,2,4,1,64,64]{4,5,3,2,1,0:T(8,128)S(1)} custom-call(f32[2,2,4,1,64,64]{5,4,3,2,1,0:T(8,128)} %get-tuple-element.8), custom_call_target="InvertDiagBlocksLowerTriangular" | custom-call | tf_op jit(solution)/shard_map/transpose(jvp(jit(cholesky)))/triangular_solve/custom-call.0 | solution.py:18
  1164.7 199.8 %all-reduce.3.cloned.1.call-done = f32[2,2,128,64,64]{4,3,2,1,0:T(8,128)} async-done(((f32[2,2,128,64,64]{4,3,2,1,0:T(8,128)}), f32[2,2,128,64,64]{4,3,2,1,0:T(8,128)}) %all-reduce.3.cloned.1.call-update) | async-done | bytes 8388624
  1364.5 2.0 fusion.26
  1366.5 1.0 fusion.68
  1367.5 0.7 fusion.24
  1368.2 2.0 fusion.37
  1370.2 1.0 fusion.9
  1371.2 0.7 fusion.7
  1371.9 1.1 fusion.4
  1373.7 1.0 fusion.20
  1374.9 1.1 fusion.64
  1376.0 1.1 convolution_add_fusion.1
  1377.1 1.0 fusion.40
  1378.1 1.0 fusion.3
  1379.3 0.9 bitcast_add_fusion
  (88 shorter events, 3.6 us)
Async XLA Ops:
  17.4 208.6 %all-to-all-start = ((bf16[256,32,448]{0,2,1:T(8,128)(2,1)}), bf16[256,32,448]{0,2,1:T(8,128)(2,1)}, u32[]{:S(2)}, u32[]{:S(2)}) async-start(bf16[256,32,448]{0,2,1:T(8,128)(2,1)} %bitcast.210), calls=%async_computation | async-start | bytes 14680064 | tf_op jit(solution)/shard_map/all_to_all | solution.py:110
  24.8 477.6 %all-gather.6.cloned.1.call-start = ((), (), s32[]{:S(2)}) async-start(), calls=%async_computation.3 | async-start | bytes 8650752 | tf_op jit(solution)/shard_map/all_gather | solution.py:108
  35.7 194.0 %copy-start.8 = (f32[2,2,4,64,64]{4,3,2,1,0:T(8,128)S(1)}, f32[2,2,4,64,64]{4,3,2,1,0:T(8,128)}, u32[]{:S(2)}) copy-start(f32[2,2,4,64,64]{4,3,2,1,0:T(8,128)} %param.13) | copy-start | bytes 786436
  226.0 334.5 %all-to-all-start.1 = ((bf16[256,32,448]{0,2,1:T(8,128)(2,1)}), bf16[256,32,448]{0,2,1:T(8,128)(2,1)}, u32[]{:S(2)}, u32[]{:S(2)}) async-start(bf16[256,32,448]{0,2,1:T(8,128)(2,1)} %bitcast.209), calls=%async_computation.1 | async-start | bytes 14680064 | tf_op jit(solution)/shard_map/all_to_all | solution.py:111
  229.7 179.8 %copy-start.23 = (s32[2,13]{1,0:T(2,128)S(1)}, s32[2,13]{1,0:T(2,128)}, u32[]{:S(2)}) copy-start(s32[2,13]{1,0:T(2,128)} %param.14) | copy-start | bytes 316
  229.7 380.2 %all-gather.4.cloned.1.call-start = ((), (), s32[]{:S(2)}) async-start(), calls=%async_computation.2 | async-start | bytes 8650752 | tf_op jit(solution)/shard_map/all_gather | solution.py:101
  230.0 179.5 %copy-start = (f32[2,2,4,64,64]{4,3,2,1,0:T(8,128)}, f32[2,2,4,64,64]{4,3,2,1,0:T(8,128)S(1)}, u32[]{:S(2)}) copy-start(f32[2,2,4,64,64]{4,3,2,1,0:T(8,128)S(1)} %bitcast_subtract_fusion.1) | copy-start | bytes 786436
  230.9 225.1 %copy-start.12 = (f32[64,64]{1,0:T(8,128)}, f32[64,64]{1,0:T(8,128)S(1)}, u32[]{:S(2)}) copy-start(f32[64,64]{1,0:T(8,128)S(1)} %get-tuple-element.21) | copy-start | bytes 49156
  324.8 1.9 copy-start.10
  325.1 1.6 copy-start.21
  325.7 1.0 copy-start.17
  405.3 50.6 %copy-start.2 = (f32[2,2,4,1,64,64]{4,5,3,2,1,0:T(8,128)}, f32[2,2,4,1,64,64]{4,5,3,2,1,0:T(8,128)S(1)}, u32[]{:S(2)}) copy-start(f32[2,2,4,1,64,64]{4,5,3,2,1,0:T(8,128)S(1)} %custom-call.22) | copy-start | bytes 786436
  407.0 0.9 copy-start.6
  409.4 955.0 %all-reduce.3.cloned.1.call-start = ((), (), s32[]{:S(2)}) async-start(), calls=%async_computation.4 | async-start | bytes 33554432
  410.2 45.7 %copy-start.14 = (s32[8192]{0:T(1024)}, s32[8192]{0:T(1024)S(1)}, u32[]{:S(2)}) copy-start(s32[8192]{0:T(1024)S(1)} %broadcast_clamp_fusion.3) | copy-start | bytes 98308
  802.0 9.5 copy-start.5
  802.0 17.7 %slice-start = ((s8[6291456]{0:T(1024)(128)(4,1)}), s8[4194304]{0:T(1024)(128)(4,1)S(1)}, s32[]{:S(2)}) async-start(s8[6291456]{0:T(1024)(128)(4,1)} %bitcast.211), calls=%async_computation.5 | async-start | bytes 8388608
  811.5 8.2 slice-start.1
  811.5 8.2 copy-start.24
  825.8 11.1 copy-start.15
  885.5 9.7 copy-start.16
  1070.3 4.6 copy-start.4
  1084.8 279.7 %copy-start.3 = (f32[2,2,4,1,64,64]{4,5,3,2,1,0:T(8,128)S(1)}, f32[2,2,4,1,64,64]{4,5,3,2,1,0:T(8,128)}, u32[]{:S(2)}) copy-start(f32[2,2,4,1,64,64]{4,5,3,2,1,0:T(8,128)} %copy-done.2) | copy-start | bytes 786436
  1084.8 281.7 %copy-start.7 = (f32[2,2,4,64,64]{4,3,2,1,0:T(8,128)S(1)}, f32[2,2,4,64,64]{4,3,2,1,0:T(8,128)}, u32[]{:S(2)}) copy-start(f32[2,2,4,64,64]{4,3,2,1,0:T(8,128)} %copy-done.6) | copy-start | bytes 786436
  1084.8 283.4 %copy-start.9 = (f32[2,2,4,64,64]{4,3,2,1,0:T(8,128)S(1)}, f32[2,2,4,64,64]{4,3,2,1,0:T(8,128)}, u32[]{:S(2)}) copy-start(f32[2,2,4,64,64]{4,3,2,1,0:T(8,128)} %get-tuple-element.15) | copy-start | bytes 786436
  1084.8 285.4 %copy-start.18 = (pred[64,64]{1,0:T(8,128)(4,1)S(1)}, pred[64,64]{1,0:T(8,128)(4,1)}, u32[]{:S(2)}) copy-start(pred[64,64]{1,0:T(8,128)(4,1)} %copy-done.17) | copy-start | bytes 12292
  1084.8 287.1 %copy-start.11 = (f32[2,2,4,64,64]{4,3,2,1,0:T(8,128)S(1)}, f32[2,2,4,64,64]{4,3,2,1,0:T(8,128)}, u32[]{:S(2)}) copy-start(f32[2,2,4,64,64]{4,3,2,1,0:T(8,128)} %copy-done.10) | copy-start | bytes 786436
  1084.8 287.1 %copy-start.22 = (pred[2,2,4]{2,1,0:T(4,128)(4,1)S(1)}, pred[2,2,4]{2,1,0:T(4,128)(4,1)}, u32[]{:S(2)}) copy-start(pred[2,2,4]{2,1,0:T(4,128)(4,1)} %copy-done.21) | copy-start | bytes 52
  1164.6 210.2 %copy-start.1 = (f32[2,2,4,64,64]{4,3,2,1,0:T(8,128)S(1)}, f32[2,2,4,64,64]{4,3,2,1,0:T(8,128)}, u32[]{:S(2)}) copy-start(f32[2,2,4,64,64]{4,3,2,1,0:T(8,128)} %copy-done) | copy-start | bytes 786436
  1164.7 210.2 %copy-start.19 = (pred[64,64]{1,0:T(8,128)(4,1)S(1)}, pred[64,64]{1,0:T(8,128)(4,1)}, u32[]{:S(2)}) copy-start(pred[64,64]{1,0:T(8,128)(4,1)} %get-tuple-element.12) | copy-start | bytes 12292
  1164.7 210.2 %copy-start.20 = (pred[64,64]{1,0:T(8,128)(4,1)S(1)}, pred[64,64]{1,0:T(8,128)(4,1)}, u32[]{:S(2)}) copy-start(pred[64,64]{1,0:T(8,128)(4,1)} %get-tuple-element.13) | copy-start | bytes 12292
  1368.2 8.9 copy-start.13
Sparse Core Ops, SparseCore 0:
  28.5 163.7 all-gather.5
  409.6 78.5 all-gather.3
  1084.9 279.4 all-reduce.2
where the time goes:
time: 1400 us; the launch traced here: 1390 us
  local copies, waits for them, and re-layouts  551 us (39%)
  waiting for transfers between devices  391 us (28%)
  other arithmetic  271 us (19%)
  matrix products  149 us (11%)
  between operations  14.9 us (1%)
    unnamed x4, waiting for transfers between devices  201 us
    all_to_all x1, waiting for transfers between devices, shards(): lax.all_to_all(gate_weight, 'rows', split_axis=1, concat_axis=0, tiled=True)  190 us
    another operation x6, other arithmetic, cayley(): lower_factor = jnp.linalg.cholesky(normal)  175 us
    gather x4, local copies, waits for them, and re-layouts, unrotate(): permuted = current[index]  154 us
    gather x4, local copies, waits for them, and re-layouts, rotate_columns(): permuted = current[index]  154 us
    another operation x1, other arithmetic, cayley(): lax.linalg.triangular_solve(lower_factor, halfway, left_side=True, lower=...  78.6 us
    gather x2, local copies, waits for them, and re-layouts, rotate_columns(): return (current[index], kept_inputs)  76.7 us
    gather x1, local copies, waits for them, and re-layouts, rotate_columns(): index = inverses[section_at][orders[section_at + 1]]  45.7 us
  transfers between devices with their start and end apart: 5, of which 2 were waited for; matrix products, arithmetic and copies ran while one was open for 34% of the time, Pallas kernels for 0%

commit v1 on v0

v1 whole, which is shorter than its diff:
```python
import jax
import jax.numpy as jnp
from jax import lax
from jax.experimental import pallas as pl
from jax.experimental.pallas import tpu as pltpu
from jax.sharding import PartitionSpec as P


def inverse_kernel(skew_ref, out_ref):
    extent = skew_ref.shape[-1]
    shape = skew_ref.shape
    row_at = lax.broadcasted_iota(jnp.int32, shape, 1)
    col_at = lax.broadcasted_iota(jnp.int32, shape, 2)
    skew = skew_ref[...]
    generator = skew - jnp.swapaxes(skew, 1, 2)
    out_ref[...] = jnp.where(row_at == col_at, 1.0, 0.0) + generator
    lane = lax.broadcasted_iota(jnp.int32, (shape[0], 1, extent), 2)

    def step(at, carry):
        work = out_ref[...]
        pivot_row = out_ref[:, pl.ds(at, 1), :]
        at_col = col_at == at
        pivot_col = jnp.sum(jnp.where(at_col, work, 0.0), axis=2, keepdims=True)
        pivot = jnp.sum(jnp.where(lane == at, pivot_row, 0.0), axis=2, keepdims=True)
        scale = 1.0 / pivot
        scaled_row = jnp.where(lane == at, 1.0, pivot_row) * scale
        cleared = jnp.where(at_col, 0.0, work)
        out_ref[...] = cleared - pivot_col * scaled_row
        out_ref[:, pl.ds(at, 1), :] = scaled_row
        return carry

    lax.fori_loop(0, extent, step, 0)


def cayley_inverse(skew_blocks):
    extent = skew_blocks.shape[-1]
    flat = skew_blocks.reshape(-1, extent, extent)
    out = pl.pallas_call(
        inverse_kernel,
        out_shape=jax.ShapeDtypeStruct(flat.shape, jnp.float32),
        in_specs=[pl.BlockSpec(memory_space=pltpu.VMEM)],
        out_specs=pl.BlockSpec(memory_space=pltpu.VMEM),
        cost_estimate=pl.CostEstimate(
            flops=50_000_000, bytes_accessed=2 * 4 * flat.size, transcendentals=0
        ),
        name="cayley_inverse",
    )(flat)
    return out.reshape(skew_blocks.shape)


def slot_order(section_row, extent):
    positions = jnp.arange(extent, dtype=jnp.int32)
    places = jnp.arange(section_row.shape[0], dtype=jnp.int32)
    digits = jnp.right_shift(positions[:, None], places[None, :]) & 1
    return jnp.sum(jnp.left_shift(digits, section_row[None, :]), axis=1)


def inverse_order(section_row, extent):
    positions = jnp.arange(extent, dtype=jnp.int32)
    places = jnp.arange(section_row.shape[0], dtype=jnp.int32)
    digits = jnp.right_shift(positions[:, None], section_row[None, :]) & 1
    return jnp.sum(jnp.left_shift(digits, places[None, :]), axis=1)


def mix(spec, blocks, columns):
    out = jnp.einsum(spec, blocks, columns, preferred_element_type=jnp.float32)
    return out.astype(jnp.bfloat16)


def shards(tokens, gate_weight, up_weight, skew_params, section_bits, upstream):
    mats, _, own_blocks, extent, _ = skew_params.shape
    model_width = tokens.shape[1]
    block_count = model_width // extent
    own_rows = gate_weight.shape[0]
    own_cols = upstream.shape[1]
    devices = gate_weight.shape[1] // own_cols
    half = devices // 2
    half_rows = half * own_rows
    side = lax.axis_index("rows") // half
    groups = [list(range(half)), list(range(half, devices))]
    swap = [(at, (at + half) % devices) for at in range(devices)]

    def move(weight):
        parts = weight.reshape(own_rows, 2, half, own_cols).transpose(2, 0, 1, 3)
        parts = parts.reshape(half, own_rows, 2 * own_cols)
        moved = lax.all_to_all(
            parts, "rows", split_axis=0, concat_axis=0, axis_index_groups=groups, tiled=True
        )
        return moved.reshape(half_rows, 2 * own_cols)

    gate_cols = move(gate_weight)
    up_cols = move(up_weight)

    inverse = cayley_inverse(skew_params)
    own_rotation = (2.0 * inverse - jnp.eye(extent, dtype=jnp.float32)).astype(jnp.bfloat16)
    packed = own_rotation.transpose(2, 3, 0, 1, 4).reshape(own_blocks * extent, -1)
    all_rotation = lax.all_gather(packed, "rows", axis=0, tiled=True)
    all_rotation = all_rotation.reshape(block_count, extent, mats, -1, extent)
    all_tokens = lax.all_gather(tokens, "rows", axis=0, tiled=True)
    token_count = all_tokens.shape[0]
    other_upstream = lax.ppermute(upstream, "rows", swap)

    order_0, order_1 = (slot_order(section_bits[at], model_width) for at in range(2))
    inverse_0, inverse_1 = (inverse_order(section_bits[at], model_width) for at in range(2))

    top_tokens = all_tokens.T[order_1].reshape(block_count, extent, token_count)
    mid = [mix("kji,kjt->kit", all_rotation[:, :, m, 1], top_tokens) for m in range(mats)]
    mid = jnp.concatenate(mid, axis=2).reshape(model_width, -1)
    mid = mid[inverse_1[order_0]].reshape(block_count, extent, mats, token_count)
    low = [mix("kji,kjt->kit", all_rotation[:, :, m, 0], mid[:, :, m]) for m in range(mats)]
    low = jnp.concatenate(low, axis=2).reshape(model_width, -1)
    own_inverse = lax.dynamic_slice(inverse_0, (side * half_rows,), (half_rows,))
    low = low[own_inverse].reshape(half_rows, mats, token_count)

    def project(at, columns):
        part = lax.dot_general(
            low[:, at], columns, (((0,), (0,)), ((), ())), preferred_element_type=jnp.float32
        )
        return part + lax.ppermute(part.astype(jnp.bfloat16), "rows", swap).astype(jnp.float32)

    gate_pre = project(0, gate_cols)
    up_pre = project(1, up_cols)
    sigmoid_val = jax.nn.sigmoid(gate_pre)
    silu_val = gate_pre * sigmoid_val
    activation = (silu_val * up_pre).astype(jnp.bfloat16)
    activation = jnp.where(side == 0, activation[:, :own_cols], activation[:, own_cols:])
    first = jnp.where(side == 0, upstream, other_upstream)
    second = jnp.where(side == 0, other_upstream, upstream)
    cotangent = jnp.concatenate([first, second], axis=1).astype(jnp.float32)
    gate_grad = (cotangent * up_pre * sigmoid_val * (1.0 + gate_pre * (1.0 - sigmoid_val))).astype(
        jnp.bfloat16
    )
    up_grad = (cotangent * silu_val).astype(jnp.bfloat16)

    pulled = [
        lax.dot_general(
            columns, grad, (((1,), (1,)), ((), ())), preferred_element_type=jnp.float32
        ).astype(jnp.bfloat16)
        for columns, grad in ((gate_cols, gate_grad), (up_cols, up_grad))
    ]
    pulled = jnp.concatenate(pulled, axis=1)
    at_row = order_0 - side * half_rows
    held = (at_row >= 0) & (at_row < half_rows)
    pulled = jnp.where(held[:, None], pulled[jnp.clip(at_row, 0, half_rows - 1)], 0)
    pulled = pulled.reshape(block_count, extent, mats, token_count)

    def total(left, right):
        terms = [
            mix("kjt,kit->kji", left[m], right[:, :, m]) for m in range(mats)
        ]
        terms = jnp.concatenate(terms, axis=2).reshape(devices, own_blocks * extent, -1)
        terms = lax.all_to_all(terms, "rows", split_axis=0, concat_axis=0, tiled=True)
        summed = jnp.sum(terms.astype(jnp.float32), axis=0)
        return summed.reshape(own_blocks, extent, mats, extent).transpose(2, 0, 1, 3)

    factor_grad_0 = total([mid[:, :, m] for m in range(mats)], pulled)
    raised = [mix("kji,kit->kjt", all_rotation[:, :, m, 0], pulled[:, :, m]) for m in range(mats)]
    raised = jnp.concatenate(raised, axis=2).reshape(model_width, -1)
    raised = raised[inverse_0[order_1]].reshape(block_count, extent, mats, token_count)
    factor_grad_1 = total([top_tokens] * mats, raised)
    factor_grad = jnp.stack([factor_grad_0, factor_grad_1], axis=1)

    left = jnp.einsum(
        "mskab,mskac->mskbc", inverse, factor_grad, precision=lax.Precision.HIGHEST
    )
    generator_grad = -2.0 * jnp.einsum(
        "mskbc,mskdc->mskbd", left, inverse, precision=lax.Precision.HIGHEST
    )
    skew_grad = generator_grad - jnp.swapaxes(generator_grad, -1, -2)
    return (activation, skew_grad)


def solution(mesh):
    placed = (
        P(("groups", "rows"), None),
        P("rows", None),
        P("rows", None),
        P(None, None, "rows", None, None),
        P(),
        P("groups", "rows"),
    )
    return jax.shard_map(
        shards,
        mesh=mesh,
        in_specs=placed,
        out_specs=(P("groups", "rows"), P("groups", None, "rows", None, None)),
        check_vma=False,
    )
```

time: 1400 us -> 1000 us (0.71)
  waiting for transfers between devices: 391 us -> 137 us
  other arithmetic: 271 us -> 59.5 us
  local copies, waits for them, and re-layouts: 551 us -> 617 us
  matrix products: 149 us -> 109 us
  starting transfers between devices: 11.2 us -> 35.8 us
  Pallas kernels: 0 us -> 19 us
    another operation x10 -> x0, other arithmetic: 268 us -> none  [the longest x6 175 us: cayley(): lower_factor = jnp.linalg.cholesky(normal)]
    unnamed x4 -> x2, waiting for transfers between devices: 201 us -> 0.71 us
    gather x12 -> x8, local copies, waits for them, and re-layouts: 476 us -> 304 us  [the longest x2 65.2 us: shards(): pulled[jnp.clip(at_row, 0, half_rows - 1)]]
    all_to_all x2 -> x4, waiting for transfers between devices: 190 us -> 51.7 us  [the longest x2 43 us: total(): lax.all_to_all(terms, 'rows', split_axis=0, concat_axis=0, tiled=True)]
    slice x0 -> x4, local copies, waits for them, and re-layouts: none -> 112 us  [the longest x1 38.8 us: total(): terms = [mix('kjt,kit->kji', left[m], right[:, :, m]) for m in range(mats)]]
    reshape x0 -> x9, local copies, waits for them, and re-layouts: none -> 78.2 us  [the longest x1 24.5 us: shards(): raised[inverse_0[order_1]].reshape(block_count, extent, mats, token_count)]
    all_gather x1, waiting for transfers between devices: 0.01 us -> 52.5 us  [shards(): all_tokens = lax.all_gather(tokens, 'rows', axis=0, tiled=True)]
    unnamed x58, local copies, waits for them, and re-layouts: 30.3 us -> 77.1 us
  transfers between devices with their start and end apart: 5 -> 9, of which waited for: 2 -> 5; matrix products, arithmetic and copies ran while one was open for 34% -> 65% of each run, Pallas kernels for 0% -> 0%
where the time goes in v1:
time: 1000 us; the launch traced here: 992 us
  local copies, waits for them, and re-layouts  617 us (62%)
  waiting for transfers between devices  137 us (14%)
  matrix products  109 us (11%)
  other arithmetic  59.5 us (6%)
  starting transfers between devices  35.8 us (4%)
  Pallas kernels  19 us (2%)
  between operations  14.7 us (1%)
    unnamed x58, local copies, waits for them, and re-layouts  77.1 us
    dot_general x10, matrix products, mix(): out = jnp.einsum(spec, blocks, columns, preferred_element_type=jnp.float32)  76.8 us
    gather x2, local copies, waits for them, and re-layouts, shards(): pulled[jnp.clip(at_row, 0, half_rows - 1)]  65.2 us
    all_gather x1, waiting for transfers between devices, shards(): all_tokens = lax.all_gather(tokens, 'rows', axis=0, tiled=True)  52.5 us
    gather x1, local copies, waits for them, and re-layouts, shards(): inverse_1[order_0]  45.5 us
    gather x1, local copies, waits for them, and re-layouts, shards(): inverse_0[order_1]  45.5 us
    gather x1, local copies, waits for them, and re-layouts, shards(): mid[inverse_1[order_0]].reshape(block_count, extent, mats, token_count)  43.3 us
    gather x1, local copies, waits for them, and re-layouts, shards(): raised[inverse_0[order_1]].reshape(block_count, extent, mats, token_count)  43.3 us
  transfers between devices with their start and end apart: 9, of which 5 were waited for; matrix products, arithmetic and copies ran while one was open for 65% of the time, Pallas kernels for 0%

profile of v1, /device:TPU:0, one launch (start us, length us, event | category | flops | bytes accessed | tf_op | source)
XLA Modules:
  0.0 992.2 jit_solution(1549220057809703330)
XLA Ops:
  7.2 19.0 %cayley_inverse.1 = f32[16,64,64]{2,1,0:T(8,128)} custom-call(f32[16,64,64]{2,1,0:T(8,128)} %bitcast.147), custom_call_target="tpu_custom_call" | custom-call | flops 50000000 | bytes 524288 | tf_op jit(solution)/shard_map/cayley_inverse/pallas_call | solution.py:38
  28.5 10.2 %copy.175 = bf16[256,14336]{0,1:T(8,128)(2,1)} copy(bf16[256,14336]{1,0:T(8,128)(2,1)} %param.7) | data formatting | bytes 14680064 | tf_op args[1]
  38.7 6.9 copy.176
  45.6 6.4 all-to-all-start
  53.0 2.7 collective-permute-start.2
  55.6 10.2 %copy.179 = bf16[256,14336]{0,1:T(8,128)(2,1)} copy(bf16[256,14336]{1,0:T(8,128)(2,1)} %param.8) | data formatting | bytes 14680064 | tf_op args[2]
  65.8 6.8 copy.180
  73.3 45.5 %gather_fusion.1 = s32[8192]{0:T(1024)S(1)} fusion(s32[8192]{0:T(1024)S(1)} %get-tuple-element.41, s32[8192]{0:T(1024)S(1)} %broadcast_clamp_fusion.3), kind=kCustom, calls=%fused_computation.1 | custom fusion | bytes 98304 | tf_op jit(solution)/shard_map/gather | solution.py:109
  118.9 45.5 %gather_fusion.5 = s32[8192]{0:T(1024)S(1)} fusion(s32[8192]{0:T(1024)S(1)} %get-tuple-element.16, s32[8192]{0:T(1024)S(1)} %broadcast_clamp_fusion.4), kind=kCustom, calls=%fused_computation.5 | custom fusion | bytes 98304 | tf_op jit(solution)/shard_map/gather | solution.py:159
  165.2 8.7 all-to-all-done
  173.8 11.3 %all-to-all-start.1 = ((bf16[16,256,896]{1,2,0:T(8,128)(2,1)}), bf16[16,256,896]{1,2,0:T(8,128)(2,1)}, u32[]{:S(2)}, u32[]{:S(2)}) async-start(bf16[16,256,896]{1,2,0:T(8,128)(2,1)} %bitcast.132), calls=%async_computation.1 | async-start | bytes 14680064 | tf_op jit(solution)/shard_map/all_to_all | solution.py:86
  187.5 15.0 %reshape.246 = bf16[128,64,2,2,64]{4,3,2,1,0:T(2,128)(2,1)} reshape(bf16[8192,256]{1,0:T(8,128)(2,1)} %all-gather.4.cloned.1.call-done) | data formatting | bytes 8388608 | tf_op jit(solution)/shard_map/reshape | solution.py:98
  202.6 27.7 %fusion.44 = (bf16[128,64,1,1,64]{4,3,2,1,0:T(2,128)(2,1)}, bf16[128,64,1,1,64]{4,3,2,1,0:T(2,128)(2,1)}, bf16[128,64,1,1,64]{4,3,2,1,0:T(2,128)(2,1)}, bf16[128,64,1,1,64]{4,3,2,1,0:T(2,128)(2,1)}) fusion(bf16[128,64,2,2,64]{4,3,2,1,0:T(2,128)(2,1)} %reshape.246), kind=kLoop, calls=%fused_computation.104 | loop fusion | bytes 8388608 | tf_op jit(solution)/shard_map/slice | solution.py:110
  230.3 8.7 copy.203
  238.9 9.2 copy.202
  248.1 9.1 copy.201
  257.2 9.1 copy.205
  266.2 52.5 %all-gather.6.cloned.1.call-done = bf16[32,12,8192]{2,1,0:T(8,128)(2,1)} async-done(((bf16[1,12,8192]{2,1,0:T(8,128)(2,1)}), bf16[32,12,8192]{2,1,0:T(8,128)(2,1)}) %all-gather.6.cloned.1.call-update) | async-done | bytes 6291472 | tf_op jit(solution)/shard_map/all_gather | solution.py:99
  318.7 8.8 reshape.245
  327.5 8.6 copy.169
  336.1 36.0 %gather_fusion = bf16[8192,384]{1,0:T(8,128)(2,1)} fusion(bf16[8192,384]{1,0:T(8,128)(2,1)} %bitcast.124, s32[8192]{0:T(1024)S(1)} %broadcast_clamp_fusion.4), kind=kCustom, calls=%fused_computation | custom fusion | bytes 12615680 | tf_op jit(solution)/shard_map/gather | solution.py:106
  372.1 4.7 convolution_convert_fusion.4
  377.4 1.8 convolution_convert_fusion.5
  379.2 5.9 pad_maximum_fusion
  385.1 43.3 %gather_fusion.2 = bf16[8192,768]{1,0:T(8,128)(2,1)} fusion(bf16[8192,768]{1,0:T(8,128)(2,1)} %bitcast.122, s32[8192]{0:T(1024)S(1)} %broadcast_clamp_fusion.2), kind=kCustom, calls=%fused_computation.2 | custom fusion | bytes 25198592 | tf_op jit(solution)/shard_map/gather | solution.py:109
  428.4 24.4 %reshape.172 = bf16[128,64,2,384]{3,2,1,0:T(2,128)(2,1)} reshape(bf16[8192,768]{1,0:T(8,128)(2,1)} %gather_fusion.2) | data formatting | bytes 25165824 | tf_op jit(solution)/shard_map/reshape | solution.py:109
  452.8 31.3 %fusion.43 = (bf16[128,64,1,384]{3,2,1,0:T(2,128)(2,1)}, bf16[128,64,1,384]{3,2,1,0:T(2,128)(2,1)S(1)}) fusion(bf16[128,64,2,384]{3,2,1,0:T(2,128)(2,1)} %reshape.172), kind=kLoop, calls=%fused_computation.103 | loop fusion | bytes 25165824 | tf_op jit(solution)/shard_map/slice | solution.py:110
  484.1 14.1 %convolution_convert_fusion.3 = bf16[128,64,384]{2,1,0:T(8,128)(2,1)} fusion(bf16[128,64,1,384]{3,2,1,0:T(2,128)(2,1)} %get-tuple-element.22, bf16[128,64,1,1,64]{1,4,0,3,2:T(8,128)(2,1)} %copy.201), kind=kOutput, calls=%fused_computation.33 | convolution fusion | flops 405798912 | bytes 13631488 | tf_op jit(solution)/shard_map/kji,kjt->kit/dot_general | solution.py:66
  498.2 6.1 convolution_convert_fusion.2
  504.3 10.7 %pad_maximum_fusion.1 = bf16[128,64,768]{2,1,0:T(8,128)(2,1)} fusion(bf16[128,64,384]{2,1,0:T(8,128)(2,1)} %convolution_convert_fusion.2, bf16[128,64,384]{2,1,0:T(8,128)(2,1)} %convolution_convert_fusion.3), kind=kLoop, calls=%fused_computation.8 | loop fusion | flops 25165824 | bytes 25165824 | tf_op jit(solution)/shard_map/concatenate | solution.py:111
  515.0 25.3 %gather_fusion.3 = bf16[4096,768]{1,0:T(8,128)(2,1)} fusion(bf16[8192,768]{1,0:T(8,128)(2,1)} %bitcast.125, s32[4096]{0:T(1024)S(1)} %fusion.36), kind=kCustom, calls=%fused_computation.3 | custom fusion | bytes 12599296 | tf_op jit(solution)/shard_map/gather | solution.py:113
  540.2 12.8 %reshape.174 = bf16[4096,2,384]{2,1,0:T(2,128)(2,1)} reshape(bf16[4096,768]{1,0:T(8,128)(2,1)} %gather_fusion.3) | data formatting | bytes 12582912 | tf_op jit(solution)/shard_map/reshape | solution.py:113
  553.0 13.9 %fusion.45 = (bf16[4096,1,384]{2,1,0:T(2,128)(2,1)}, bf16[4096,1,384]{2,1,0:T(2,128)(2,1)}) fusion(bf16[4096,2,384]{2,1,0:T(2,128)(2,1)} %reshape.174), kind=kLoop, calls=%fused_computation.105 | loop fusion | bytes 12582912 | tf_op jit(solution)/shard_map/slice | solution.py:117
  566.9 11.2 %copy.177 = bf16[16,256,896]{2,1,0:T(8,128)(2,1)} copy(bf16[16,256,896]{1,2,0:T(8,128)(2,1)} %all-to-all-done) | data formatting | bytes 14680064 | tf_op jit(solution)/shard_map/all_to_all | solution.py:86
  578.1 8.1 fusion.47
  586.3 5.1 collective-permute-start
  591.4 11.2 %copy.181 = bf16[16,256,896]{2,1,0:T(8,128)(2,1)} copy(bf16[16,256,896]{1,2,0:T(8,128)(2,1)} %all-to-all-done.1) | data formatting | bytes 14680064 | tf_op jit(solution)/shard_map/all_to_all | solution.py:86
  602.6 9.8 fusion.46
  612.8 24.2 %collective-permute-done = bf16[384,896]{1,0:T(8,128)(2,1)S(1)} collective-permute-done((bf16[384,896]{1,0:T(8,128)(2,1)S(1)}, bf16[384,896]{1,0:T(8,128)(2,1)S(1)}, u32[]{:S(2)}, u32[]{:S(2)}) %collective-permute-start) | collective-permute-done | bytes 688160 | tf_op jit(solution)/shard_map/ppermute | solution.py:119
  637.9 5.4 fusion.7
  643.3 8.1 collective-permute-done.1
  652.3 6.6 fusion.6
  658.9 3.1 pad_maximum_fusion.3
  662.1 8.7 copy.185
  670.7 40.7 %gather_fusion.4 = bf16[8192,768]{1,0:T(8,128)(2,1)} fusion(bf16[4096,768]{1,0:T(8,128)(2,1)} %copy.185, s32[8192]{0:T(1024)S(1)} %copy-done.16), kind=kCustom, calls=%fused_computation.4 | custom fusion | bytes 25198592 | tf_op jit(solution)/shard_map/gather | solution.py:144
  711.4 24.6 %gather.33 = bf16[128,64,2,384]{3,2,1,0:T(2,128)(2,1)} reshape(bf16[8192,768]{1,0:T(8,128)(2,1)} %gather_fusion.4) | data formatting | bytes 25165824 | tf_op jit(solution)/shard_map/gather | solution.py:144
  736.0 12.6 %copy_select_fusion = bf16[128,64,2,384]{3,1,0,2:T(8,128)(2,1)} fusion(bf16[128,64,2,384]{3,2,1,0:T(2,128)(2,1)} %gather.33, pred[128,64]{1,0:T(8,128)(4,1)S(1)} %copy-done.18), kind=kLoop, calls=%fused_computation.10 | loop fusion | flops 6291456 | bytes 25174016 | tf_op jit(solution)/shard_map/jit(_where)/select_n | solution.py:144
  748.6 10.1 %fusion.19 = bf16[128,64,64]{2,1,0:T(8,128)(2,1)} fusion(bf16[128,64,2,384]{3,1,0,2:T(8,128)(2,1)} %copy_select_fusion, bf16[128,64,1,384]{3,2,1,0:T(2,128)(2,1)} %get-tuple-element.22), kind=kOutput, calls=%fused_computation.49 | convolution fusion | flops 403177472 | bytes 19922944 | tf_op jit(solution)/shard_map/kjt,kit->kji/dot_general | solution.py:66
  758.6 10.2 %fusion.18 = bf16[128,64,64]{2,1,0:T(8,128)(2,1)} fusion(bf16[128,64,2,384]{3,1,0,2:T(8,128)(2,1)} %copy_select_fusion, bf16[128,64,1,384]{3,2,1,0:T(2,128)(2,1)} %copy-done.1), kind=kOutput, calls=%fused_computation.48 | convolution fusion | flops 403177472 | bytes 19922944 | tf_op jit(solution)/shard_map/kjt,kit->kji/dot_general | solution.py:66
  768.8 7.4 fusion.9
  776.2 7.4 fusion.8
  783.6 2.5 pad_maximum_fusion.4
  786.2 3.9 all-to-all-start.2
  790.1 10.7 %pad_maximum_fusion.2 = bf16[128,64,768]{2,1,0:T(8,128)(2,1)} fusion(bf16[128,64,384]{2,1,0:T(8,128)(2,1)} %fusion.8, bf16[128,64,384]{2,1,0:T(8,128)(2,1)} %fusion.9), kind=kLoop, calls=%fused_computation.9 | loop fusion | flops 25165824 | bytes 25165824 | tf_op jit(solution)/shard_map/concatenate | solution.py:158
  800.7 43.3 %gather_fusion.6 = bf16[8192,768]{1,0:T(8,128)(2,1)} fusion(bf16[8192,768]{1,0:T(8,128)(2,1)} %bitcast.123, s32[8192]{0:T(1024)S(1)} %copy-done.17), kind=kCustom, calls=%fused_computation.6 | custom fusion | bytes 25198592 | tf_op jit(solution)/shard_map/gather | solution.py:159
  844.0 24.5 %reshape.184 = bf16[128,64,2,384]{3,2,1,0:T(2,128)(2,1)} reshape(bf16[8192,768]{1,0:T(8,128)(2,1)} %gather_fusion.6) | data formatting | bytes 25165824 | tf_op jit(solution)/shard_map/reshape | solution.py:159
  868.5 38.8 %fusion.42 = (bf16[128,64,1,384]{3,2,1,0:T(2,128)(2,1)}, bf16[128,64,1,384]{3,2,1,0:T(2,128)(2,1)}) fusion(bf16[128,64,2,384]{3,2,1,0:T(2,128)(2,1)} %reshape.184), kind=kLoop, calls=%fused_computation.102 | loop fusion | bytes 25165824 | tf_op jit(solution)/shard_map/slice | solution.py:149
  907.4 6.9 fusion.20
  914.3 8.2 fusion.21
  922.5 4.2 pad_maximum_fusion.5
  926.7 5.9 all-to-all-start.3
  932.6 2.5 multiply_convert_fusion
  936.2 1.9 convert_reduce_fusion.1
  938.5 43.0 %all-to-all-done.3 = bf16[32,256,128]{2,1,0:T(8,128)(2,1)S(1)} async-done(((bf16[32,256,128]{2,1,0:T(8,128)(2,1)}), bf16[32,256,128]{2,1,0:T(8,128)(2,1)S(1)}, u32[]{:S(2)}, u32[]{:S(2)}) %all-to-all-start.3) | async-done | bytes 2097184 | tf_op jit(solution)/shard_map/all_to_all | solution.py:152
  (90 shorter events, 14.8 us)
Async XLA Ops:
  7.2 180.4 %all-gather.4.cloned.1.call-start = ((), (), s32[]{:S(2)}) async-start(), calls=%async_computation.4 | async-start | bytes 4325376 | tf_op jit(solution)/shard_map/all_gather | solution.py:97
  45.6 7.2 copy-start.15
  45.6 128.2 %all-to-all-start = ((bf16[16,256,896]{1,2,0:T(8,128)(2,1)}), bf16[16,256,896]{1,2,0:T(8,128)(2,1)}, u32[]{:S(2)}, u32[]{:S(2)}) async-start(bf16[16,256,896]{1,2,0:T(8,128)(2,1)} %bitcast.133), calls=%async_computation | async-start | bytes 14680064 | tf_op jit(solution)/shard_map/all_to_all | solution.py:86
  52.0 266.7 %all-gather.6.cloned.1.call-start = ((), (), s32[]{:S(2)}) async-start(), calls=%async_computation.5 | async-start | bytes 8650752 | tf_op jit(solution)/shard_map/all_gather | solution.py:99
  53.0 133.6 %collective-permute-start.2 = (bf16[384,448]{1,0:T(8,128)(2,1)S(1)}, bf16[384,448]{1,0:T(8,128)(2,1)S(1)}, u32[]{:S(2)}, u32[]{:S(2)}) collective-permute-start(bf16[384,448]{1,0:T(8,128)(2,1)S(1)} %copy.183), channel_id=1, source_target_pairs={{0,16},{1,17},{2,18},{3,19},{4,20},{5,21},{6,22},{7,23},{8,24},{9,... | collective-permute-start | bytes 1032200 | tf_op jit(solution)/shard_map/ppermute | solution.py:101
  65.8 6.8 copy-start.19
  173.8 417.5 %all-to-all-start.1 = ((bf16[16,256,896]{1,2,0:T(8,128)(2,1)}), bf16[16,256,896]{1,2,0:T(8,128)(2,1)}, u32[]{:S(2)}, u32[]{:S(2)}) async-start(bf16[16,256,896]{1,2,0:T(8,128)(2,1)} %bitcast.132), calls=%async_computation.1 | async-start | bytes 14680064 | tf_op jit(solution)/shard_map/all_to_all | solution.py:86
  372.1 4.7 copy-start
  372.1 5.2 copy-start.4
  484.1 14.1 %copy-start.1 = (bf16[128,64,1,384]{3,2,1,0:T(2,128)(2,1)}, bf16[128,64,1,384]{3,2,1,0:T(2,128)(2,1)S(1)}, u32[]{:S(2)}) copy-start(bf16[128,64,1,384]{3,2,1,0:T(2,128)(2,1)S(1)} %get-tuple-element.23) | copy-start | bytes 18874372
  586.3 66.1 %copy-start.9 = (f32[384,896]{1,0:T(8,128)}, f32[384,896]{1,0:T(8,128)S(1)}, u32[]{:S(2)}) copy-start(f32[384,896]{1,0:T(8,128)S(1)} %get-tuple-element.39) | copy-start | bytes 4128772
  586.3 50.8 %collective-permute-start = (bf16[384,896]{1,0:T(8,128)(2,1)S(1)}, bf16[384,896]{1,0:T(8,128)(2,1)S(1)}, u32[]{:S(2)}, u32[]{:S(2)}) collective-permute-start(bf16[384,896]{1,0:T(8,128)(2,1)S(1)} %get-tuple-element.38), channel_id=1, source_target_pairs={{0,16},{1,17},{2,18},{3,19},{4,20},{5,21},{6,22},{7,23},{8,24},{9,... | collective-permute-start | bytes 2064392 | tf_op jit(solution)/shard_map/ppermute | solution.py:119
  602.6 35.4 %copy-start.6 = (bf16[16,256,896]{2,1,0:T(8,128)(2,1)S(1)}, bf16[16,256,896]{2,1,0:T(8,128)(2,1)}, u32[]{:S(2)}) copy-start(bf16[16,256,896]{2,1,0:T(8,128)(2,1)} %copy.181) | copy-start | bytes 22020100
  602.6 35.4 %copy-start.13 = (bf16[384,448]{1,0:T(8,128)(2,1)S(1)}, bf16[384,448]{1,0:T(8,128)(2,1)}, u32[]{:S(2)}) copy-start(bf16[384,448]{1,0:T(8,128)(2,1)} %get-tuple-element.30) | copy-start | bytes 1032196
  602.6 35.4 %copy-start.14 = (bf16[384,448]{1,0:T(8,128)(2,1)S(1)}, bf16[384,448]{1,0:T(8,128)(2,1)}, u32[]{:S(2)}) copy-start(bf16[384,448]{1,0:T(8,128)(2,1)} %get-tuple-element.31) | copy-start | bytes 1032196
  602.6 49.8 %slice-start.2 = ((s8[7340032]{0:T(1024)(128)(4,1)}), s8[4194304]{0:T(1024)(128)(4,1)S(1)}, s32[]{:S(2)}) async-start(s8[7340032]{0:T(1024)(128)(4,1)} %bitcast.140), calls=%async_computation.8 | async-start | bytes 8388608
  612.4 39.1 %collective-permute-start.1 = (bf16[384,896]{1,0:T(8,128)(2,1)}, bf16[384,896]{1,0:T(8,128)(2,1)S(1)}, u32[]{:S(2)}, u32[]{:S(2)}) collective-permute-start(bf16[384,896]{1,0:T(8,128)(2,1)} %get-tuple-element.36), channel_id=1, source_target_pairs={{0,16},{1,17},{2,18},{3,19},{4,20},{5,21},{6,22},{7,23},{8,24},{9,... | collective-permute-start | bytes 2064392 | tf_op jit(solution)/shard_map/ppermute | solution.py:119
  637.1 0.9 copy-start.10
  637.9 14.4 %slice-start.3 = ((s8[7340032]{0:T(1024)(128)(4,1)}), s8[3145728]{0:T(1024)(128)(4,1)S(1)}, s32[]{:S(2)}) async-start(s8[7340032]{0:T(1024)(128)(4,1)} %bitcast.140), calls=%async_computation.9 | async-start | bytes 6291456
  651.5 0.9 copy-start.12
  662.1 8.7 copy-start.16
  711.4 24.6 %copy-start.18 = (pred[128,64]{1,0:T(8,128)(4,1)S(1)}, pred[128,64]{1,0:T(8,128)(4,1)}, u32[]{:S(2)}) copy-start(pred[128,64]{1,0:T(8,128)(4,1)} %and.33) | copy-start | bytes 24580
  758.6 10.2 %copy-start.2 = (bf16[128,64,1,1,64]{1,4,0,3,2:T(8,128)(2,1)S(1)}, bf16[128,64,1,1,64]{1,4,0,3,2:T(8,128)(2,1)}, u32[]{:S(2)}) copy-start(bf16[128,64,1,1,64]{1,4,0,3,2:T(8,128)(2,1)} %copy.201) | copy-start | bytes 3145732
  768.8 7.4 copy-start.3
  776.2 7.5 copy-start.7
  776.2 7.5 copy-start.8
  786.2 140.5 %all-to-all-start.2 = ((bf16[32,256,128]{2,1,0:T(8,128)(2,1)}), bf16[32,256,128]{2,1,0:T(8,128)(2,1)}, u32[]{:S(2)}, u32[]{:S(2)}) async-start(bf16[32,256,128]{2,1,0:T(8,128)(2,1)} %bitcast.37), calls=%async_computation.2 | async-start | bytes 4194304 | tf_op jit(solution)/shard_map/all_to_all | solution.py:152
  790.1 10.7 %copy-start.17 = (s32[8192]{0:T(1024)S(1)}, s32[8192]{0:T(1024)}, u32[]{:S(2)}) copy-start(s32[8192]{0:T(1024)} %broadcast_clamp_fusion.1) | copy-start | bytes 98308
  844.0 63.3 %slice-start = ((s8[6291456]{0:T(1024)(128)(4,1)}), s8[2097152]{0:T(1024)(128)(4,1)S(1)}, s32[]{:S(2)}) async-start(s8[6291456]{0:T(1024)(128)(4,1)} %bitcast.128), calls=%async_computation.6 | async-start | bytes 4194304
  868.5 38.8 %slice-start.1 = ((s8[6291456]{0:T(1024)(128)(4,1)}), s8[4194304]{0:T(1024)(128)(4,1)S(1)}, s32[]{:S(2)}) async-start(s8[6291456]{0:T(1024)(128)(4,1)} %bitcast.128), calls=%async_computation.7 | async-start | bytes 8388608
  922.5 10.1 %copy-start.11 = (bf16[384,896]{1,0:T(8,128)(2,1)S(1)}, bf16[384,896]{1,0:T(8,128)(2,1)}, u32[]{:S(2)}) copy-start(bf16[384,896]{1,0:T(8,128)(2,1)} %copy-done.10) | copy-start | bytes 2064388
  926.7 54.8 %all-to-all-start.3 = ((bf16[32,256,128]{2,1,0:T(8,128)(2,1)}), bf16[32,256,128]{2,1,0:T(8,128)(2,1)S(1)}, u32[]{:S(2)}, u32[]{:S(2)}) async-start(bf16[32,256,128]{2,1,0:T(8,128)(2,1)} %bitcast.45), calls=%async_computation.3 | async-start | bytes 4194304 | tf_op jit(solution)/shard_map/all_to_all | solution.py:152
  932.6 49.5 %copy-start.5 = (f32[16,64,64]{2,1,0:T(8,128)S(1)}, f32[16,64,64]{2,1,0:T(8,128)}, u32[]{:S(2)}) copy-start(f32[16,64,64]{2,1,0:T(8,128)} %cayley_inverse.1) | copy-start | bytes 786436
Sparse Core Ops, SparseCore 0:
  28.6 115.1 all-gather.3
  146.7 172.0 all-gather.5

commit v2 on v1

v2 whole, which is shorter than its diff:
```python
import jax
import jax.numpy as jnp
from jax import lax
from jax.experimental import pallas as pl
from jax.experimental.pallas import tpu as pltpu
from jax.sharding import PartitionSpec as P


def inverse_kernel(skew_ref, out_ref):
    extent = skew_ref.shape[-1]
    shape = skew_ref.shape
    row_at = lax.broadcasted_iota(jnp.int32, shape, 1)
    col_at = lax.broadcasted_iota(jnp.int32, shape, 2)
    skew = skew_ref[...]
    generator = skew - jnp.swapaxes(skew, 1, 2)
    out_ref[...] = jnp.where(row_at == col_at, 1.0, 0.0) + generator
    lane = lax.broadcasted_iota(jnp.int32, (shape[0], 1, extent), 2)

    def step(at, carry):
        work = out_ref[...]
        pivot_row = out_ref[:, pl.ds(at, 1), :]
        at_col = col_at == at
        pivot_col = jnp.sum(jnp.where(at_col, work, 0.0), axis=2, keepdims=True)
        pivot = jnp.sum(jnp.where(lane == at, pivot_row, 0.0), axis=2, keepdims=True)
        scale = 1.0 / pivot
        scaled_row = jnp.where(lane == at, 1.0, pivot_row) * scale
        cleared = jnp.where(at_col, 0.0, work)
        out_ref[...] = cleared - pivot_col * scaled_row
        out_ref[:, pl.ds(at, 1), :] = scaled_row
        return carry

    lax.fori_loop(0, extent, step, 0)


def cayley_inverse(skew_blocks):
    extent = skew_blocks.shape[-1]
    flat = skew_blocks.reshape(-1, extent, extent)
    out = pl.pallas_call(
        inverse_kernel,
        out_shape=jax.ShapeDtypeStruct(flat.shape, jnp.float32),
        in_specs=[pl.BlockSpec(memory_space=pltpu.VMEM)],
        out_specs=pl.BlockSpec(memory_space=pltpu.VMEM),
        cost_estimate=pl.CostEstimate(
            flops=50_000_000, bytes_accessed=2 * 4 * flat.size, transcendentals=0
        ),
        name="cayley_inverse",
    )(flat)
    return out.reshape(skew_blocks.shape)


def estimate(flops, *arrays):
    moved = sum(array.size * array.dtype.itemsize for array in arrays)
    return pl.CostEstimate(flops=flops, bytes_accessed=moved, transcendentals=0)


def pack(weight, half, cols):
    rows, width = weight.shape
    step = min(rows, 32)

    def body(in_ref, out_ref):
        for at in range(half):
            left = in_ref[:, at * cols : (at + 1) * cols]
            right = in_ref[:, (half + at) * cols : (half + at + 1) * cols]
            out_ref[at] = jnp.concatenate([left, right], axis=1)

    out = jax.ShapeDtypeStruct((half, rows, 2 * cols), weight.dtype)
    return pl.pallas_call(
        body,
        out_shape=out,
        grid=(rows // step,),
        in_specs=[pl.BlockSpec((step, width), lambda at: (at, 0))],
        out_specs=pl.BlockSpec((half, step, 2 * cols), lambda at: (0, at, 0)),
        cost_estimate=estimate(0, weight, out),
        name="pack",
    )(weight)


def blocked(body, name, extent, inputs, out_widths):
    rows = inputs[0].shape[0]
    step = min(8 * extent, rows)
    outs = tuple(jax.ShapeDtypeStruct((rows, width), jnp.bfloat16) for width in out_widths)
    return pl.pallas_call(
        body,
        out_shape=outs,
        grid=(rows // step,),
        in_specs=[pl.BlockSpec((step, array.shape[1]), lambda at: (at, 0)) for array in inputs],
        out_specs=tuple(pl.BlockSpec((step, width), lambda at: (at, 0)) for width in out_widths),
        cost_estimate=estimate(4 * rows * extent * out_widths[-1], *inputs, *outs),
        name=name,
    )(*inputs)


def dot(left, right, left_dim, right_dim):
    contract = (((left_dim,), (right_dim,)), ((), ()))
    return lax.dot_general(left, right, contract, preferred_element_type=jnp.float32)


def mix(rotation, columns, section, extent, mats, count):
    shared = columns.shape[1] == count
    pair = mats * extent

    def body(rotation_ref, in_ref, out_ref):
        for at in range(in_ref.shape[0] // extent):
            rows = slice(at * extent, (at + 1) * extent)
            blocks = rotation_ref[rows, section * pair : (section + 1) * pair]
            if shared:
                mixed = dot(blocks, in_ref[rows, :], 0, 0).astype(jnp.bfloat16)
            for m in range(mats):
                lanes = slice(m * count, (m + 1) * count)
                if shared:
                    out_ref[rows, lanes] = mixed[m * extent : (m + 1) * extent]
                else:
                    own = blocks[:, m * extent : (m + 1) * extent]
                    out_ref[rows, lanes] = dot(own, in_ref[rows, lanes], 0, 0).astype(jnp.bfloat16)

    return blocked(body, "mix", extent, (rotation, columns), (mats * count,))[0]


def raise_terms(rotation, left, right, extent, mats, count):
    def body(rotation_ref, left_ref, right_ref, terms_ref, out_ref):
        for at in range(left_ref.shape[0] // extent):
            rows = slice(at * extent, (at + 1) * extent)
            terms = []
            for m in range(mats):
                lanes = slice(m * count, (m + 1) * count)
                pulled = right_ref[rows, lanes]
                terms.append(dot(left_ref[rows, lanes], pulled, 1, 1))
                own = rotation_ref[rows, m * extent : (m + 1) * extent]
                out_ref[rows, lanes] = dot(own, pulled, 1, 0).astype(jnp.bfloat16)
            terms_ref[rows, :] = jnp.concatenate(terms, axis=1).astype(jnp.bfloat16)

    return blocked(
        body, "raise_terms", extent, (rotation, left, right), (mats * extent, mats * count)
    )


def top_terms(left, right, extent, mats, count):
    def body(left_ref, right_ref, terms_ref):
        for at in range(left_ref.shape[0] // extent):
            rows = slice(at * extent, (at + 1) * extent)
            terms = [
                dot(left_ref[rows, :], right_ref[rows, m * count : (m + 1) * count], 1, 1)
                for m in range(mats)
            ]
            terms_ref[rows, :] = jnp.concatenate(terms, axis=1).astype(jnp.bfloat16)

    return blocked(body, "top_terms", extent, (left, right), (mats * extent,))[0]


def pull(gate_cols, up_cols, gate_grad, up_grad):
    rows, width = gate_cols.shape
    count = gate_grad.shape[0]
    step = min(512, rows)
    last = rows // step - 1

    def body(gate_ref, up_ref, gate_grad_ref, up_grad_ref, out_ref):
        @pl.when(pl.program_id(0) <= last)
        def _():
            out_ref[:, :count] = dot(gate_ref[...], gate_grad_ref[...], 1, 1).astype(jnp.bfloat16)
            out_ref[:, count:] = dot(up_ref[...], up_grad_ref[...], 1, 1).astype(jnp.bfloat16)

        @pl.when(pl.program_id(0) > last)
        def _():
            out_ref[...] = jnp.zeros_like(out_ref)

    out = jax.ShapeDtypeStruct((rows + step, 2 * count), jnp.bfloat16)
    weights = pl.BlockSpec((step, width), lambda at: (jnp.minimum(at, last), 0))
    grads = pl.BlockSpec((count, width), lambda at: (0, 0))
    return pl.pallas_call(
        body,
        out_shape=out,
        grid=(last + 2,),
        in_specs=[weights, weights, grads, grads],
        out_specs=pl.BlockSpec((step, 2 * count), lambda at: (at, 0)),
        cost_estimate=estimate(4 * rows * width * count, gate_cols, up_cols, out),
        name="pull",
    )(gate_cols, up_cols, gate_grad, up_grad)


def slot_order(section_row, positions):
    places = jnp.arange(section_row.shape[0], dtype=jnp.int32)
    digits = jnp.right_shift(positions[:, None], places[None, :]) & 1
    return jnp.sum(jnp.left_shift(digits, section_row[None, :]), axis=1)


def places_of(bits, section_row):
    places = jnp.arange(section_row.shape[0], dtype=jnp.int32)
    found = bits[:, None] == section_row[None, :]
    return jnp.sum(jnp.where(found, places[None, :], 0), axis=1)


def take(array, index):
    return array.at[index].get(mode="promise_in_bounds")


def shards(tokens, gate_weight, up_weight, skew_params, section_bits, upstream):
    mats, _, own_blocks, extent, _ = skew_params.shape
    model_width = tokens.shape[1]
    own_rows = gate_weight.shape[0]
    own_cols = upstream.shape[1]
    devices = gate_weight.shape[1] // own_cols
    half = devices // 2
    half_rows = half * own_rows
    side = lax.axis_index("rows") // half
    groups = [list(range(half)), list(range(half, devices))]
    swap = [(at, (at + half) % devices) for at in range(devices)]

    def move(parts):
        moved = lax.all_to_all(
            parts, "rows", split_axis=0, concat_axis=0, axis_index_groups=groups, tiled=True
        )
        return moved.reshape(half_rows, 2 * own_cols)

    all_tokens = lax.all_gather(tokens, "rows", axis=0, tiled=True)
    token_count = all_tokens.shape[0]
    gate_parts, skew_params = lax.optimization_barrier(
        (pack(gate_weight, half, own_cols), skew_params)
    )
    gate_cols = move(gate_parts)
    up_cols = move(pack(up_weight, half, own_cols))

    inverse = cayley_inverse(skew_params)
    own_rotation = (2.0 * inverse - jnp.eye(extent, dtype=jnp.float32)).astype(jnp.bfloat16)
    packed = own_rotation.transpose(2, 3, 1, 0, 4).reshape(own_blocks * extent, -1)
    packed, all_tokens = lax.optimization_barrier((packed, all_tokens))
    rotation = lax.all_gather(packed, "rows", axis=0, tiled=True)
    other_upstream = lax.ppermute(upstream, "rows", swap)

    positions = jnp.arange(model_width, dtype=jnp.int32)
    bits_0, bits_1 = section_bits[0], section_bits[1]
    order_0 = slot_order(bits_0, positions)
    order_1 = slot_order(bits_1, positions)
    one_to_zero = slot_order(places_of(bits_0, bits_1), positions)
    zero_to_one = slot_order(places_of(bits_1, bits_0), positions)
    natural = jnp.arange(bits_0.shape[0], dtype=jnp.int32)
    own_positions = side * half_rows + jnp.arange(half_rows, dtype=jnp.int32)
    own_inverse = slot_order(places_of(natural, bits_0), own_positions)

    sizes = (extent, mats, token_count)
    top_tokens = take(all_tokens.T, order_1)
    mid = take(mix(rotation, top_tokens, 1, *sizes), one_to_zero)
    low = take(mix(rotation, mid, 0, *sizes), own_inverse)

    def project(at, columns):
        part = dot(low[:, at * token_count : (at + 1) * token_count], columns, 0, 0)
        return part + lax.ppermute(part.astype(jnp.bfloat16), "rows", swap).astype(jnp.float32)

    gate_pre = project(0, gate_cols)
    up_pre = project(1, up_cols)
    sigmoid_val = jax.nn.sigmoid(gate_pre)
    silu_val = gate_pre * sigmoid_val
    activation = (silu_val * up_pre).astype(jnp.bfloat16)
    activation = jnp.where(side == 0, activation[:, :own_cols], activation[:, own_cols:])
    first = jnp.where(side == 0, upstream, other_upstream)
    second = jnp.where(side == 0, other_upstream, upstream)
    cotangent = jnp.concatenate([first, second], axis=1).astype(jnp.float32)
    gate_grad = (cotangent * up_pre * sigmoid_val * (1.0 + gate_pre * (1.0 - sigmoid_val))).astype(
        jnp.bfloat16
    )
    up_grad = (cotangent * silu_val).astype(jnp.bfloat16)

    at_row = order_0 - side * half_rows
    held = (at_row >= 0) & (at_row < half_rows)
    pulled = take(pull(gate_cols, up_cols, gate_grad, up_grad), jnp.where(held, at_row, half_rows))

    def total(terms):
        terms = terms.reshape(devices, own_blocks * extent, -1)
        terms = lax.all_to_all(terms, "rows", split_axis=0, concat_axis=0, tiled=True)
        summed = jnp.sum(terms.astype(jnp.float32), axis=0)
        return summed.reshape(own_blocks, extent, mats, extent).transpose(2, 0, 1, 3)

    terms_0, raised = raise_terms(rotation, mid, pulled, *sizes)
    factor_grad_0 = total(terms_0)
    raised = take(raised, zero_to_one)
    factor_grad_1 = total(top_terms(top_tokens, raised, *sizes))
    factor_grad = jnp.stack([factor_grad_0, factor_grad_1], axis=1)

    left = jnp.einsum(
        "mskab,mskac->mskbc", inverse, factor_grad, precision=lax.Precision.HIGHEST
    )
    generator_grad = -2.0 * jnp.einsum(
        "mskbc,mskdc->mskbd", left, inverse, precision=lax.Precision.HIGHEST
    )
    skew_grad = generator_grad - jnp.swapaxes(generator_grad, -1, -2)
    return (activation, skew_grad)


def solution(mesh):
    placed = (
        P(("groups", "rows"), None),
        P("rows", None),
        P("rows", None),
        P(None, None, "rows", None, None),
        P(),
        P("groups", "rows"),
    )
    return jax.shard_map(
        shards,
        mesh=mesh,
        in_specs=placed,
        out_specs=(P("groups", "rows"), P("groups", None, "rows", None, None)),
        check_vma=False,
    )
```

time: 1000 us -> 739 us (0.74)
  local copies, waits for them, and re-layouts: 617 us -> 210 us
  waiting for transfers between devices: 137 us -> 274 us
  Pallas kernels: 19 us -> 125 us
  matrix products: 109 us -> 17.4 us
  blocking collectives: 0 us -> 52.1 us
  other arithmetic: 59.5 us -> 10.6 us
    gather x8 -> x5, local copies, waits for them, and re-layouts: 304 us -> 189 us  [take(): return array.at[index].get(mode='promise_in_bounds')]
    slice x4 -> x0, local copies, waits for them, and re-layouts: 112 us -> none  [the longest x1 38.8 us: total(): terms = [mix('kjt,kit->kji', left[m], right[:, :, m]) for m in range(mats)]]
    pallas_call x0 -> x7, Pallas kernels: none -> 106 us  [the longest x4 73.6 us: blocked(): pl.pallas_call(body, out_shape=outs, grid=(rows // step,), in_specs=[pl.B...]
    all_to_all x2, waiting for transfers between devices: 8.7 us -> 114 us  [move(): lax.all_to_all(parts, 'rows', split_axis=0, concat_axis=0, axis_index_gro...]
    dot_general x14 -> x2, matrix products: 107 us -> 15.4 us  [dot(): lax.dot_general(left, right, contract, preferred_element_type=jnp.float32)]
    reshape x5 -> x1, local copies, waits for them, and re-layouts: 77.6 us -> 0.87 us  [shards(): own_rotation.transpose(2, 3, 1, 0, 4).reshape(own_blocks * extent, -1)]
    unnamed x58 -> x10, local copies, waits for them, and re-layouts: 77.1 us -> 2.11 us
    all_gather x1, waiting for transfers between devices: 0.01 us -> 63.3 us  [shards(): rotation = lax.all_gather(packed, 'rows', axis=0, tiled=True)]
  transfers between devices with their start and end apart: 9 -> 8, of which waited for: 5 -> 5; matrix products, arithmetic and copies ran while one was open for 65% -> 20% of each run, Pallas kernels for 0% -> 8%
where the time goes in v2:
time: 739 us; the launch traced here: 735 us
  waiting for transfers between devices  274 us (37%)
  local copies, waits for them, and re-layouts  210 us (28%)
  Pallas kernels  125 us (17%)
  blocking collectives  52.1 us (7%)
  starting transfers between devices  31.5 us (4%)
  matrix products  17.4 us (2%)
  between operations  14.3 us (2%)
  other arithmetic  10.6 us (1%)
    gather x5, local copies, waits for them, and re-layouts, take(): return array.at[index].get(mode='promise_in_bounds')  189 us
    all_to_all x2, waiting for transfers between devices, move(): lax.all_to_all(parts, 'rows', split_axis=0, concat_axis=0, axis_index_gro...  114 us
    pallas_call x4, Pallas kernels, blocked(): pl.pallas_call(body, out_shape=outs, grid=(rows // step,), in_specs=[pl.B...  73.6 us
    all_gather x1, waiting for transfers between devices, shards(): rotation = lax.all_gather(packed, 'rows', axis=0, tiled=True)  63.3 us
    all_to_all x1, blocking collectives, total(): lax.all_to_all(terms, 'rows', split_axis=0, concat_axis=0, tiled=True)  52.1 us
    ppermute x2, waiting for transfers between devices, project(): lax.ppermute(part.astype(jnp.bfloat16), 'rows', swap).astype(jnp.float32)  51.8 us
    all_to_all x1, waiting for transfers between devices, total(): lax.all_to_all(terms, 'rows', split_axis=0, concat_axis=0, tiled=True)  43.8 us
    all_to_all x2, starting transfers between devices, move(): lax.all_to_all(parts, 'rows', split_axis=0, concat_axis=0, axis_index_gro...  22.2 us
  transfers between devices with their start and end apart: 8, of which 5 were waited for; matrix products, arithmetic and copies ran while one was open for 20% of the time, Pallas kernels for 8%

profile of v2, /device:TPU:0, one launch (start us, length us, event | category | flops | bytes accessed | tf_op | source)
XLA Modules:
  0.0 735.3 jit_solution(3217373057115935317)
XLA Ops:
  7.2 9.0 %pack.2 = bf16[16,256,896]{2,1,0:T(8,128)(2,1)} custom-call(bf16[256,14336]{1,0:T(8,128)(2,1)} %in_ref.2), custom_call_target="tpu_custom_call" | custom-call | bytes 14680064 | tf_op jit(solution)/shard_map/pack/pallas_call | solution.py:67
  16.2 6.3 all-to-all-start
  22.5 0.0 all-gather.6.cloned.1.call-start
  22.6 0.7 all-gather.6.cloned.1.call-update
  23.2 9.0 %pack.3 = bf16[16,256,896]{2,1,0:T(8,128)(2,1)} custom-call(bf16[256,14336]{1,0:T(8,128)(2,1)} %in_ref.3), custom_call_target="tpu_custom_call" | custom-call | bytes 14680064 | tf_op jit(solution)/shard_map/pack/pallas_call | solution.py:67
  32.3 0.0 copy-start.3
  32.3 114.3 %all-to-all-done = bf16[16,256,896]{2,1,0:T(8,128)(2,1)} async-done(((bf16[16,256,896]{2,1,0:T(8,128)(2,1)}), bf16[16,256,896]{2,1,0:T(8,128)(2,1)}, u32[]{:S(2)}, u32[]{:S(2)}) %all-to-all-start) | async-done | bytes 7340064 | tf_op jit(solution)/shard_map/all_to_all | solution.py:209
  146.5 15.9 %all-to-all-start.1 = ((bf16[16,256,896]{2,1,0:T(8,128)(2,1)}), bf16[16,256,896]{2,1,0:T(8,128)(2,1)}, u32[]{:S(2)}, u32[]{:S(2)}) async-start(bf16[16,256,896]{2,1,0:T(8,128)(2,1)} %pack.3), calls=%async_computation.1 | async-start | bytes 14680064 | tf_op jit(solution)/shard_map/all_to_all | solution.py:209
  162.4 0.0 all-gather.4.cloned.1.call-start
  162.5 0.0 copy-done.2
  162.5 0.2 copy.43
  162.7 2.4 collective-permute-start.2
  165.1 19.0 %cayley_inverse.1 = f32[16,64,64]{2,1,0:T(8,128)} custom-call(f32[16,64,64]{2,1,0:T(8,128)} %bitcast.49), custom_call_target="tpu_custom_call" | custom-call | flops 50000000 | bytes 524288 | tf_op jit(solution)/shard_map/cayley_inverse/pallas_call | solution.py:38
  184.0 1.1 fusion.13
  185.1 0.3 copy.40
  185.4 0.9 reshape.132
  186.3 0.0 copy-done.3
  186.3 0.2 select_reduce_fusion
  186.5 0.1 shift-left_reduce_fusion.4
  186.6 0.3 shift-left_reduce_fusion.1
  187.0 0.0 all-gather.6.cloned.1.call-done
  187.0 8.8 %reshape.180 = bf16[384,8192]{1,0:T(8,128)(2,1)} reshape(bf16[32,12,8192]{2,1,0:T(8,128)(2,1)} %all-gather.6.cloned.1.call-done) | data formatting | bytes 12582912 | tf_op jit(solution)/shard_map/optimization_barrier | solution.py:225
  195.8 0.0 all-gather.4.cloned.1.call-update
  195.8 0.3 shift-left_reduce_fusion
  196.3 0.1 compare_select_fusion.1
  196.4 8.7 %copy.41 = bf16[384,8192]{0,1:T(8,128)(2,1)} copy(bf16[384,8192]{1,0:T(8,128)(2,1)} %reshape.180) | data formatting | bytes 12582912 | tf_op jit(solution)/shard_map/optimization_barrier | solution.py:225
  205.1 36.1 %gather_fusion = bf16[8192,384]{1,0:T(8,128)(2,1)} fusion(bf16[8192,384]{1,0:T(8,128)(2,1)} %bitcast.41, s32[8192]{0:T(1024)S(1)} %broadcast_clamp_fusion.3), kind=kCustom, calls=%fused_computation | custom fusion | bytes 12615680 | tf_op jit(solution)/shard_map/gather | solution.py:193
  241.2 63.3 %all-gather.4.cloned.1.call-done.rotation_ref = bf16[8192,256]{1,0:T(8,128)(2,1)} async-done(((bf16[256,256]{1,0:T(8,128)(2,1)}), bf16[8192,256]{1,0:T(8,128)(2,1)}) %all-gather.4.cloned.1.call-update) | async-done | bytes 4194320 | tf_op jit(solution)/shard_map/all_gather | solution.py:226
  304.5 15.8 %mix.2 = bf16[8192,768]{1,0:T(8,128)(2,1)} custom-call(bf16[8192,256]{1,0:T(8,128)(2,1)} %all-gather.4.cloned.1.call-done.rotation_ref, bf16[8192,384]{1,0:T(8,128)(2,1)} %gather_fusion), custom_call_target="tpu_custom_call" | custom-call | flops 1610612736 | bytes 23068672 | tf_op jit(solution)/shard_map/mix/pallas_call | solution.py:82
  320.2 43.3 %gather_fusion.1 = bf16[8192,768]{1,0:T(8,128)(2,1)} fusion(bf16[8192,768]{1,0:T(8,128)(2,1)} %mix.2, s32[8192]{0:T(1024)S(1)} %broadcast_clamp_fusion.2), kind=kCustom, calls=%fused_computation.1 | custom fusion | bytes 25198592 | tf_op jit(solution)/shard_map/gather | solution.py:193
  363.5 18.6 %mix.3 = bf16[8192,768]{1,0:T(8,128)(2,1)} custom-call(bf16[8192,256]{1,0:T(8,128)(2,1)} %all-gather.4.cloned.1.call-done.rotation_ref, bf16[8192,768]{1,0:T(8,128)(2,1)} %gather_fusion.1), custom_call_target="tpu_custom_call" | custom-call | flops 1610612736 | bytes 29360128 | tf_op jit(solution)/shard_map/mix/pallas_call | solution.py:82
  382.1 25.2 %gather_fusion.2 = bf16[4096,768]{1,0:T(8,128)(2,1)} fusion(bf16[8192,768]{1,0:T(8,128)(2,1)} %mix.3, s32[4096]{0:T(1024)S(1)} %broadcast_clamp_fusion.4), kind=kCustom, calls=%fused_computation.2 | custom fusion | bytes 12599296 | tf_op jit(solution)/shard_map/gather | solution.py:193
  407.4 8.3 %fusion.16 = (bf16[384,896]{1,0:T(8,128)(2,1)}, f32[384,896]{1,0:T(8,128)S(1)}) fusion(bf16[4096,896]{1,0:T(8,128)(2,1)} %bitcast.13.gate_ref, bf16[4096,768]{1,0:T(8,128)(2,1)} %gather_fusion.2), kind=kOutput, calls=%fused_computation.64 | convolution fusion | flops 2818916352 | bytes 12550144 | tf_op jit(solution)/shard_map/dot_general | solution.py:95
  415.7 1.6 collective-permute-start
  417.3 0.0 all-to-all-done.1
  417.3 7.1 fusion.17
  424.4 1.4 collective-permute-start.1
  425.8 0.0 collective-permute-done.2
  425.8 1.1 broadcast_select_fusion.1
  426.9 37.7 %collective-permute-done = bf16[384,896]{1,0:T(8,128)(2,1)S(1)} collective-permute-done((bf16[384,896]{1,0:T(8,128)(2,1)}, bf16[384,896]{1,0:T(8,128)(2,1)S(1)}, u32[]{:S(2)}, u32[]{:S(2)}) %collective-permute-start) | collective-permute-done | bytes 688160 | tf_op jit(solution)/shard_map/ppermute | solution.py:246
  464.6 0.0 copy-start.1
  464.6 14.1 %collective-permute-done.1 = bf16[384,896]{1,0:T(8,128)(2,1)S(1)} collective-permute-done((bf16[384,896]{1,0:T(8,128)(2,1)S(1)}, bf16[384,896]{1,0:T(8,128)(2,1)S(1)}, u32[]{:S(2)}, u32[]{:S(2)}) %collective-permute-start.1) | collective-permute-done | bytes 688160 | tf_op jit(solution)/shard_map/ppermute | solution.py:246
  478.7 0.0 copy-done.1
  478.7 3.2 fusion.6
  481.9 14.7 %pull.1 = bf16[4608,768]{1,0:T(8,128)(2,1)} custom-call(bf16[4096,896]{1,0:T(8,128)(2,1)} %bitcast.13.gate_ref, bf16[4096,896]{1,0:T(8,128)(2,1)} %bitcast.14.up_ref, bf16[384,896]{1,0:T(8,128)(2,1)} %get-tuple-element.27.gate_grad_ref, bf16[384,896]{1,0:T(8,128)(2,1)} %get-tuple-element.29.up_grad_ref), custom_call_target="tpu_custom_call" | custom-call | flops 5637144576 | bytes 21757952 | tf_op jit(solution)/shard_map/pull/pallas_call | solution.py:169
  496.6 41.0 %gather_fusion.3 = bf16[8192,768]{1,0:T(8,128)(2,1)} fusion(bf16[4608,768]{1,0:T(8,128)(2,1)} %pull.1, s32[8192]{0:T(1024)S(1)} %broadcast_clamp_fusion), kind=kCustom, calls=%fused_computation.3 | custom fusion | bytes 25198592 | tf_op jit(solution)/shard_map/gather | solution.py:193
  537.6 23.1 %raise_terms.1 = (bf16[8192,128]{1,0:T(8,128)(2,1)}, bf16[8192,768]{1,0:T(8,128)(2,1)}) custom-call(bf16[8192,256]{1,0:T(8,128)(2,1)} %all-gather.4.cloned.1.call-done.rotation_ref, bf16[8192,768]{1,0:T(8,128)(2,1)} %gather_fusion.1, bf16[8192,768]{1,0:T(8,128)(2,1)} %gather_fusion.3), custom_call_target="tpu_custom_call" | custom-call | flops 1610612736 | bytes 44040192 | tf_op jit(solution)/shard_map/raise_terms/pallas_call | solution.py:82
  560.7 43.3 %gather_fusion.4 = bf16[8192,768]{1,0:T(8,128)(2,1)} fusion(bf16[8192,768]{1,0:T(8,128)(2,1)} %get-tuple-element.13, s32[8192]{0:T(1024)S(1)} %broadcast_clamp_fusion.1), kind=kCustom, calls=%fused_computation.4 | custom fusion | bytes 25198592 | tf_op jit(solution)/shard_map/gather | solution.py:193
  604.0 16.1 %top_terms.1 = bf16[8192,128]{1,0:T(8,128)(2,1)} custom-call(bf16[8192,384]{1,0:T(8,128)(2,1)} %gather_fusion, bf16[8192,768]{1,0:T(8,128)(2,1)} %gather_fusion.4), custom_call_target="tpu_custom_call" | custom-call | flops 268435456 | bytes 20971520 | tf_op jit(solution)/shard_map/top_terms/pallas_call | solution.py:82
  620.2 52.1 %all_to_all.20 = bf16[32,256,128]{2,1,0:T(8,128)(2,1)} all-to-all(bf16[32,256,128]{2,1,0:T(8,128)(2,1)} %bitcast.42), channel_id=1, replica_groups=mesh['groups'=1,'rows'=32] {'rows'}, dimensions={0} | all-to-all | bytes 4194304 | tf_op jit(solution)/shard_map/all_to_all | solution.py:268
  672.3 0.0 copy-start
  672.3 3.8 all-to-all-start.2
  676.1 0.9 slice_select_fusion
  677.1 1.9 copy.49
  679.0 1.9 convert_reduce_fusion
  680.9 0.2 reshape.138
  681.1 43.8 %all-to-all-done.2 = bf16[32,256,128]{2,1,0:T(8,128)(2,1)S(1)} async-done(((bf16[32,256,128]{2,1,0:T(8,128)(2,1)}), bf16[32,256,128]{2,1,0:T(8,128)(2,1)S(1)}, u32[]{:S(2)}, u32[]{:S(2)}) %all-to-all-start.2) | async-done | bytes 2097184 | tf_op jit(solution)/shard_map/all_to_all | solution.py:268
  724.9 0.3 convert_reduce_fusion.1
  725.2 0.2 reshape.136
  725.4 0.0 copy-done
  725.4 1.0 fusion.9
  726.4 1.0 convolution_multiply_fusion
  727.4 0.2 copy.48
  727.6 0.9 bitcast_subtract_fusion
  (16 shorter events, 0.2 us)
Async XLA Ops:
  16.2 130.4 %all-to-all-start = ((bf16[16,256,896]{2,1,0:T(8,128)(2,1)}), bf16[16,256,896]{2,1,0:T(8,128)(2,1)}, u32[]{:S(2)}, u32[]{:S(2)}) async-start(bf16[16,256,896]{2,1,0:T(8,128)(2,1)} %pack.2), calls=%async_computation | async-start | bytes 14680064 | tf_op jit(solution)/shard_map/all_to_all | solution.py:209
  22.5 164.5 %all-gather.6.cloned.1.call-start = ((), (), s32[]{:S(2)}) async-start(), calls=%async_computation.5 | async-start | bytes 8650752 | tf_op jit(solution)/shard_map/all_gather | solution.py:214
  32.3 130.2 %copy-start.2 = (bf16[384,448]{0,1:T(8,128)(2,1)S(1)}, bf16[384,448]{0,1:T(8,128)(2,1)}, u32[]{:S(2)}) copy-start(bf16[384,448]{0,1:T(8,128)(2,1)} %param.11) | copy-start | bytes 1032196
  32.3 154.0 %copy-start.3 = (s32[2,13]{1,0:T(2,128)S(1)}, s32[2,13]{1,0:T(2,128)}, u32[]{:S(2)}) copy-start(s32[2,13]{1,0:T(2,128)} %param.10) | copy-start | bytes 316
  146.5 270.8 %all-to-all-start.1 = ((bf16[16,256,896]{2,1,0:T(8,128)(2,1)}), bf16[16,256,896]{2,1,0:T(8,128)(2,1)}, u32[]{:S(2)}, u32[]{:S(2)}) async-start(bf16[16,256,896]{2,1,0:T(8,128)(2,1)} %pack.3), calls=%async_computation.1 | async-start | bytes 14680064 | tf_op jit(solution)/shard_map/all_to_all | solution.py:209
  162.4 142.0 %all-gather.4.cloned.1.call-start = ((), (), s32[]{:S(2)}) async-start(), calls=%async_computation.4 | async-start | bytes 4325376 | tf_op jit(solution)/shard_map/all_gather | solution.py:226
  162.7 263.1 %collective-permute-start.2 = (bf16[384,448]{1,0:T(8,128)(2,1)S(1)}, bf16[384,448]{1,0:T(8,128)(2,1)}, u32[]{:S(2)}, u32[]{:S(2)}) collective-permute-start(bf16[384,448]{1,0:T(8,128)(2,1)S(1)} %copy.43), channel_id=1, source_target_pairs={{0,16},{1,17},{2,18},{3,19},{4,20},{5,21},{6,22},{7,23},{8,24},{9,... | collective-permute-start | bytes 1032200 | tf_op jit(solution)/shard_map/ppermute | solution.py:227
  415.7 48.9 %collective-permute-start = (bf16[384,896]{1,0:T(8,128)(2,1)}, bf16[384,896]{1,0:T(8,128)(2,1)S(1)}, u32[]{:S(2)}, u32[]{:S(2)}) collective-permute-start(bf16[384,896]{1,0:T(8,128)(2,1)} %get-tuple-element.34), channel_id=1, source_target_pairs={{0,16},{1,17},{2,18},{3,19},{4,20},{5,21},{6,22},{7,23},{8,24},{9,... | collective-permute-start | bytes 2064392 | tf_op jit(solution)/shard_map/ppermute | solution.py:246
  424.4 54.3 %collective-permute-start.1 = (bf16[384,896]{1,0:T(8,128)(2,1)S(1)}, bf16[384,896]{1,0:T(8,128)(2,1)S(1)}, u32[]{:S(2)}, u32[]{:S(2)}) collective-permute-start(bf16[384,896]{1,0:T(8,128)(2,1)S(1)} %get-tuple-element.36), channel_id=1, source_target_pairs={{0,16},{1,17},{2,18},{3,19},{4,20},{5,21},{6,22},{7,23},{8,24},{9,... | collective-permute-start | bytes 2064392 | tf_op jit(solution)/shard_map/ppermute | solution.py:246
  464.6 14.1 %copy-start.1 = (bf16[384,896]{1,0:T(8,128)(2,1)}, bf16[384,896]{1,0:T(8,128)(2,1)S(1)}, u32[]{:S(2)}) copy-start(bf16[384,896]{1,0:T(8,128)(2,1)S(1)} %collective-permute-done) | copy-start | bytes 2064388
  672.3 53.1 %copy-start = (f32[16,64,64]{2,1,0:T(8,128)S(1)}, f32[16,64,64]{2,1,0:T(8,128)}, u32[]{:S(2)}) copy-start(f32[16,64,64]{2,1,0:T(8,128)} %cayley_inverse.1) | copy-start | bytes 786436
  672.3 52.6 %all-to-all-start.2 = ((bf16[32,256,128]{2,1,0:T(8,128)(2,1)}), bf16[32,256,128]{2,1,0:T(8,128)(2,1)S(1)}, u32[]{:S(2)}, u32[]{:S(2)}) async-start(bf16[32,256,128]{2,1,0:T(8,128)(2,1)} %bitcast.46), calls=%async_computation.2 | async-start | bytes 4194304 | tf_op jit(solution)/shard_map/all_to_all | solution.py:268
Sparse Core Ops, SparseCore 0:
  26.2 135.5 all-gather.5
  195.9 108.4 all-gather.3

commit v3 on v2

--- a/solution.py
+++ b/solution.py
@@ -213,16 +213,13 @@
 
     all_tokens = lax.all_gather(tokens, "rows", axis=0, tiled=True)
     token_count = all_tokens.shape[0]
-    gate_parts, skew_params = lax.optimization_barrier(
-        (pack(gate_weight, half, own_cols), skew_params)
-    )
-    gate_cols = move(gate_parts)
-    up_cols = move(pack(up_weight, half, own_cols))
-
     inverse = cayley_inverse(skew_params)
     own_rotation = (2.0 * inverse - jnp.eye(extent, dtype=jnp.float32)).astype(jnp.bfloat16)
     packed = own_rotation.transpose(2, 3, 1, 0, 4).reshape(own_blocks * extent, -1)
-    packed, all_tokens = lax.optimization_barrier((packed, all_tokens))
+    packed, gate_parts, all_tokens = lax.optimization_barrier(
+        (packed, pack(gate_weight, half, own_cols), all_tokens)
+    )
+    gate_cols = move(gate_parts)
     rotation = lax.all_gather(packed, "rows", axis=0, tiled=True)
     other_upstream = lax.ppermute(upstream, "rows", swap)
 
@@ -237,7 +234,10 @@
     own_inverse = slot_order(places_of(natural, bits_0), own_positions)
 
     sizes = (extent, mats, token_count)
-    top_tokens = take(all_tokens.T, order_1)
+    top_tokens, up_parts, rotation = lax.optimization_barrier(
+        (take(all_tokens.T, order_1), pack(up_weight, half, own_cols), rotation)
+    )
+    up_cols = move(up_parts)
     mid = take(mix(rotation, top_tokens, 1, *sizes), one_to_zero)
     low = take(mix(rotation, mid, 0, *sizes), own_inverse)
 
@@ -263,17 +263,18 @@
     held = (at_row >= 0) & (at_row < half_rows)
     pulled = take(pull(gate_cols, up_cols, gate_grad, up_grad), jnp.where(held, at_row, half_rows))
 
-    def total(terms):
+    def send(terms):
         terms = terms.reshape(devices, own_blocks * extent, -1)
-        terms = lax.all_to_all(terms, "rows", split_axis=0, concat_axis=0, tiled=True)
+        return lax.all_to_all(terms, "rows", split_axis=0, concat_axis=0, tiled=True)
+
+    def summed_of(terms):
         summed = jnp.sum(terms.astype(jnp.float32), axis=0)
         return summed.reshape(own_blocks, extent, mats, extent).transpose(2, 0, 1, 3)
 
     terms_0, raised = raise_terms(rotation, mid, pulled, *sizes)
-    factor_grad_0 = total(terms_0)
-    raised = take(raised, zero_to_one)
-    factor_grad_1 = total(top_terms(top_tokens, raised, *sizes))
-    factor_grad = jnp.stack([factor_grad_0, factor_grad_1], axis=1)
+    sent_0, raised = lax.optimization_barrier((send(terms_0), take(raised, zero_to_one)))
+    sent_1 = send(top_terms(top_tokens, raised, *sizes))
+    factor_grad = jnp.stack([summed_of(sent_0), summed_of(sent_1)], axis=1)
 
     left = jnp.einsum(
         "mskab,mskac->mskbc", inverse, factor_grad, precision=lax.Precision.HIGHEST

time: 739 us -> 633 us (0.86)
  blocking collectives: 52.1 us -> 0 us
  waiting for transfers between devices: 274 us -> 227 us
  starting transfers between devices: 31.5 us -> 21.5 us
    all_to_all x2, waiting for transfers between devices: 114 us -> 0.01 us  [move(): lax.all_to_all(parts, 'rows', split_axis=0, concat_axis=0, axis_index_gro...]
    all_gather x1, waiting for transfers between devices: 0.02 us -> 52.9 us  [shards(): all_tokens = lax.all_gather(tokens, 'rows', axis=0, tiled=True)]
    all_to_all x1 -> x0, blocking collectives: 52.1 us -> none  [total(): lax.all_to_all(terms, 'rows', split_axis=0, concat_axis=0, tiled=True)]
    all_to_all x2, starting transfers between devices: 22.2 us -> 9.63 us  [move(): lax.all_to_all(parts, 'rows', split_axis=0, concat_axis=0, axis_index_gro...]
    all_to_all x1 -> x2, waiting for transfers between devices: 43.8 us -> 50.8 us  [send(): lax.all_to_all(terms, 'rows', split_axis=0, concat_axis=0, tiled=True)]
  transfers between devices with their start and end apart: 8 -> 9, of which waited for: 5 -> 6; matrix products, arithmetic and copies ran while one was open for 20% -> 29% of each run, Pallas kernels for 8% -> 11%
where the time goes in v3:
time: 633 us; the launch traced here: 630 us
  waiting for transfers between devices  227 us (36%)
  local copies, waits for them, and re-layouts  211 us (33%)
  Pallas kernels  125 us (20%)
  starting transfers between devices  21.5 us (3%)
  matrix products  19.1 us (3%)
  between operations  14.3 us (2%)
  other arithmetic  11.2 us (2%)
    gather x5, local copies, waits for them, and re-layouts, take(): return array.at[index].get(mode='promise_in_bounds')  190 us
    pallas_call x4, Pallas kernels, blocked(): pl.pallas_call(body, out_shape=outs, grid=(rows // step,), in_specs=[pl.B...  73.6 us
    all_gather x1, waiting for transfers between devices, shards(): rotation = lax.all_gather(packed, 'rows', axis=0, tiled=True)  66.5 us
    ppermute x2, waiting for transfers between devices, project(): lax.ppermute(part.astype(jnp.bfloat16), 'rows', swap).astype(jnp.float32)  55.7 us
    all_gather x1, waiting for transfers between devices, shards(): all_tokens = lax.all_gather(tokens, 'rows', axis=0, tiled=True)  52.9 us
    all_to_all x2, waiting for transfers between devices, send(): lax.all_to_all(terms, 'rows', split_axis=0, concat_axis=0, tiled=True)  50.8 us
    pallas_call x1, Pallas kernels, cayley_inverse(): pl.pallas_call(inverse_kernel, out_shape=jax.ShapeDtypeStruct(flat.shape,...  19 us
    pallas_call x2, Pallas kernels, pack(): pl.pallas_call(body, out_shape=out, grid=(rows // step,), in_specs=[pl.Bl...  18.1 us
  transfers between devices with their start and end apart: 9, of which 6 were waited for; matrix products, arithmetic and copies ran while one was open for 29% of the time, Pallas kernels for 11%

profile of v3, /device:TPU:0, one launch (start us, length us, event | category | flops | bytes accessed | tf_op | source)
XLA Modules:
  0.0 629.9 jit_solution(10678832101523767882)
XLA Ops:
  7.2 0.0 all-gather.6.cloned.1.call-start
  7.2 0.7 all-gather.6.cloned.1.call-update
  7.9 19.0 %cayley_inverse.1 = f32[16,64,64]{2,1,0:T(8,128)} custom-call(f32[16,64,64]{2,1,0:T(8,128)} %bitcast.45), custom_call_target="tpu_custom_call" | custom-call | flops 50000000 | bytes 524288 | tf_op jit(solution)/shard_map/cayley_inverse/pallas_call | solution.py:38
  26.9 1.1 fusion.13
  28.0 0.3 copy.40
  28.3 0.9 reshape.132
  29.1 9.0 %pack.2 = bf16[16,256,896]{2,1,0:T(8,128)(2,1)} custom-call(bf16[256,14336]{1,0:T(8,128)(2,1)} %in_ref.2), custom_call_target="tpu_custom_call" | custom-call | bytes 14680064 | tf_op jit(solution)/shard_map/pack/pallas_call | solution.py:67
  38.1 52.9 %all-gather.6.cloned.1.call-done = bf16[32,12,8192]{2,1,0:T(8,128)(2,1)} async-done(((bf16[1,12,8192]{2,1,0:T(8,128)(2,1)}), bf16[32,12,8192]{2,1,0:T(8,128)(2,1)}) %all-gather.6.cloned.1.call-update) | async-done | bytes 6291472 | tf_op jit(solution)/shard_map/all_gather | solution.py:214
  91.1 8.8 %reshape.180 = bf16[384,8192]{1,0:T(8,128)(2,1)} reshape(bf16[32,12,8192]{2,1,0:T(8,128)(2,1)} %all-gather.6.cloned.1.call-done) | data formatting | bytes 12582912 | tf_op jit(solution)/shard_map/optimization_barrier | solution.py:219
  99.8 4.8 all-to-all-start
  104.6 0.0 all-gather.4.cloned.1.call-start
  104.6 0.7 all-gather.4.cloned.1.call-update
  105.3 0.0 copy-start.3
  105.3 9.1 %pack.3 = bf16[16,256,896]{2,1,0:T(8,128)(2,1)} custom-call(bf16[256,14336]{1,0:T(8,128)(2,1)} %in_ref.3), custom_call_target="tpu_custom_call" | custom-call | bytes 14680064 | tf_op jit(solution)/shard_map/pack/pallas_call | solution.py:67
  114.4 0.0 copy-done.3
  114.4 0.3 shift-left_reduce_fusion.1
  114.8 8.7 %copy.41 = bf16[384,8192]{0,1:T(8,128)(2,1)} copy(bf16[384,8192]{1,0:T(8,128)(2,1)} %reshape.180) | data formatting | bytes 12582912 | tf_op jit(solution)/shard_map/optimization_barrier | solution.py:219
  123.5 36.2 %gather_fusion = bf16[8192,384]{1,0:T(8,128)(2,1)} fusion(bf16[8192,384]{1,0:T(8,128)(2,1)} %bitcast.37, s32[8192]{0:T(1024)S(1)} %broadcast_clamp_fusion.3), kind=kCustom, calls=%fused_computation | custom fusion | bytes 12615680 | tf_op jit(solution)/shard_map/gather | solution.py:193
  159.7 66.5 %all-gather.4.cloned.1.call-done.rotation_ref = bf16[8192,256]{1,0:T(8,128)(2,1)} async-done(((bf16[256,256]{1,0:T(8,128)(2,1)}), bf16[8192,256]{1,0:T(8,128)(2,1)}) %all-gather.4.cloned.1.call-update) | async-done | bytes 4194320 | tf_op jit(solution)/shard_map/all_gather | solution.py:223
  226.2 0.0 all-to-all-done
  226.2 4.9 all-to-all-start.1
  231.1 0.0 copy-done.2
  231.1 0.2 copy.43
  231.3 2.1 collective-permute-start.2
  233.4 0.2 select_reduce_fusion
  233.6 0.1 shift-left_reduce_fusion.4
  233.7 0.3 shift-left_reduce_fusion
  234.2 15.8 %mix.2 = bf16[8192,768]{1,0:T(8,128)(2,1)} custom-call(bf16[8192,256]{1,0:T(8,128)(2,1)} %all-gather.4.cloned.1.call-done.rotation_ref, bf16[8192,384]{1,0:T(8,128)(2,1)} %gather_fusion), custom_call_target="tpu_custom_call" | custom-call | flops 1610612736 | bytes 23068672 | tf_op jit(solution)/shard_map/mix/pallas_call | solution.py:82
  250.0 43.5 %gather_fusion.1 = bf16[8192,768]{1,0:T(8,128)(2,1)} fusion(bf16[8192,768]{1,0:T(8,128)(2,1)} %mix.2, s32[8192]{0:T(1024)S(1)} %broadcast_clamp_fusion.2), kind=kCustom, calls=%fused_computation.1 | custom fusion | bytes 25198592 | tf_op jit(solution)/shard_map/gather | solution.py:193
  293.4 18.6 %mix.3 = bf16[8192,768]{1,0:T(8,128)(2,1)} custom-call(bf16[8192,256]{1,0:T(8,128)(2,1)} %all-gather.4.cloned.1.call-done.rotation_ref, bf16[8192,768]{1,0:T(8,128)(2,1)} %gather_fusion.1), custom_call_target="tpu_custom_call" | custom-call | flops 1610612736 | bytes 29360128 | tf_op jit(solution)/shard_map/mix/pallas_call | solution.py:82
  312.1 25.3 %gather_fusion.2 = bf16[4096,768]{1,0:T(8,128)(2,1)} fusion(bf16[8192,768]{1,0:T(8,128)(2,1)} %mix.3, s32[4096]{0:T(1024)S(1)} %broadcast_clamp_fusion.4), kind=kCustom, calls=%fused_computation.2 | custom fusion | bytes 12599296 | tf_op jit(solution)/shard_map/gather | solution.py:193
  337.4 8.3 %fusion.16 = (bf16[384,896]{1,0:T(8,128)(2,1)}, f32[384,896]{1,0:T(8,128)S(1)}) fusion(bf16[4096,896]{1,0:T(8,128)(2,1)} %bitcast.13.gate_ref, bf16[4096,768]{1,0:T(8,128)(2,1)} %gather_fusion.2), kind=kOutput, calls=%fused_computation.62 | convolution fusion | flops 2818916352 | bytes 12550144 | tf_op jit(solution)/shard_map/dot_general | solution.py:95
  345.7 0.9 collective-permute-start
  346.6 0.0 all-to-all-done.1
  346.6 8.8 %fusion.17 = (bf16[384,896]{1,0:T(8,128)(2,1)}, f32[384,896]{1,0:T(8,128)}) fusion(bf16[4096,896]{1,0:T(8,128)(2,1)} %bitcast.14.up_ref, bf16[4096,768]{1,0:T(8,128)(2,1)} %gather_fusion.2), kind=kOutput, calls=%fused_computation.63 | convolution fusion | flops 2818916352 | bytes 12550144 | tf_op jit(solution)/shard_map/dot_general | solution.py:95
  355.4 2.0 collective-permute-start.1
  357.4 0.1 compare_select_fusion.1
  357.5 0.0 collective-permute-done.2
  357.5 1.1 broadcast_select_fusion.1
  358.6 40.9 %collective-permute-done = bf16[384,896]{1,0:T(8,128)(2,1)S(1)} collective-permute-done((bf16[384,896]{1,0:T(8,128)(2,1)}, bf16[384,896]{1,0:T(8,128)(2,1)S(1)}, u32[]{:S(2)}, u32[]{:S(2)}) %collective-permute-start) | collective-permute-done | bytes 688160 | tf_op jit(solution)/shard_map/ppermute | solution.py:246
  399.5 14.8 %collective-permute-done.1 = bf16[384,896]{1,0:T(8,128)(2,1)} collective-permute-done((bf16[384,896]{1,0:T(8,128)(2,1)}, bf16[384,896]{1,0:T(8,128)(2,1)}, u32[]{:S(2)}, u32[]{:S(2)}) %collective-permute-start.1) | collective-permute-done | bytes 688160 | tf_op jit(solution)/shard_map/ppermute | solution.py:246
  414.2 0.0 copy-done.1
  414.2 3.9 fusion.6
  418.1 14.7 %pull.1 = bf16[4608,768]{1,0:T(8,128)(2,1)} custom-call(bf16[4096,896]{1,0:T(8,128)(2,1)} %bitcast.13.gate_ref, bf16[4096,896]{1,0:T(8,128)(2,1)} %bitcast.14.up_ref, bf16[384,896]{1,0:T(8,128)(2,1)} %get-tuple-element.35.gate_grad_ref, bf16[384,896]{1,0:T(8,128)(2,1)} %get-tuple-element.37.up_grad_ref), custom_call_target="tpu_custom_call" | custom-call | flops 5637144576 | bytes 21757952 | tf_op jit(solution)/shard_map/pull/pallas_call | solution.py:169
  432.8 41.1 %gather_fusion.3 = bf16[8192,768]{1,0:T(8,128)(2,1)} fusion(bf16[4608,768]{1,0:T(8,128)(2,1)} %pull.1, s32[8192]{0:T(1024)S(1)} %broadcast_clamp_fusion), kind=kCustom, calls=%fused_computation.3 | custom fusion | bytes 25198592 | tf_op jit(solution)/shard_map/gather | solution.py:193
  473.9 23.1 %raise_terms.1 = (bf16[8192,128]{1,0:T(8,128)(2,1)}, bf16[8192,768]{1,0:T(8,128)(2,1)}) custom-call(bf16[8192,256]{1,0:T(8,128)(2,1)} %all-gather.4.cloned.1.call-done.rotation_ref, bf16[8192,768]{1,0:T(8,128)(2,1)} %gather_fusion.1, bf16[8192,768]{1,0:T(8,128)(2,1)} %gather_fusion.3), custom_call_target="tpu_custom_call" | custom-call | flops 1610612736 | bytes 44040192 | tf_op jit(solution)/shard_map/raise_terms/pallas_call | solution.py:82
  497.1 2.7 all-to-all-start.2
  499.9 43.5 %gather_fusion.4 = bf16[8192,768]{1,0:T(8,128)(2,1)} fusion(bf16[8192,768]{1,0:T(8,128)(2,1)} %get-tuple-element.19, s32[8192]{0:T(1024)S(1)} %broadcast_clamp_fusion.1), kind=kCustom, calls=%fused_computation.4 | custom fusion | bytes 25198592 | tf_op jit(solution)/shard_map/gather | solution.py:193
  543.3 5.4 all-to-all-done.2
  548.7 16.1 %top_terms.1 = bf16[8192,128]{1,0:T(8,128)(2,1)} custom-call(bf16[8192,384]{1,0:T(8,128)(2,1)} %gather_fusion, bf16[8192,768]{1,0:T(8,128)(2,1)} %gather_fusion.4), custom_call_target="tpu_custom_call" | custom-call | flops 268435456 | bytes 20971520 | tf_op jit(solution)/shard_map/top_terms/pallas_call | solution.py:82
  564.9 4.0 all-to-all-start.3
  568.9 0.9 slice_select_fusion
  569.8 1.9 copy.49
  571.7 0.3 convert_reduce_fusion.1
  572.0 0.2 reshape.136
  572.2 0.1 copy.45
  572.3 45.4 %all-to-all-done.3 = bf16[32,256,128]{2,1,0:T(8,128)(2,1)} async-done(((bf16[32,256,128]{2,1,0:T(8,128)(2,1)}), bf16[32,256,128]{2,1,0:T(8,128)(2,1)}, u32[]{:S(2)}, u32[]{:S(2)}) %all-to-all-start.3) | async-done | bytes 2097184 | tf_op jit(solution)/shard_map/all_to_all | solution.py:268
  617.7 1.9 convert_reduce_fusion
  619.6 0.2 reshape.138
  619.8 0.1 copy.46
  620.0 1.0 fusion.9
  621.0 1.0 convolution_multiply_fusion
  622.0 0.2 copy.48
  622.2 0.9 bitcast_subtract_fusion
  (17 shorter events, 0.2 us)
Async XLA Ops:
  7.2 83.9 %all-gather.6.cloned.1.call-start = ((), (), s32[]{:S(2)}) async-start(), calls=%async_computation.5 | async-start | bytes 8650752 | tf_op jit(solution)/shard_map/all_gather | solution.py:214
  99.8 126.4 %all-to-all-start = ((bf16[16,256,896]{2,1,0:T(8,128)(2,1)}), bf16[16,256,896]{2,1,0:T(8,128)(2,1)}, u32[]{:S(2)}, u32[]{:S(2)}) async-start(bf16[16,256,896]{2,1,0:T(8,128)(2,1)} %pack.2), calls=%async_computation | async-start | bytes 14680064 | tf_op jit(solution)/shard_map/all_to_all | solution.py:209
  104.6 121.6 %all-gather.4.cloned.1.call-start = ((), (), s32[]{:S(2)}) async-start(), calls=%async_computation.4 | async-start | bytes 4325376 | tf_op jit(solution)/shard_map/all_gather | solution.py:223
  105.3 9.1 %copy-start.3 = (s32[2,13]{1,0:T(2,128)S(1)}, s32[2,13]{1,0:T(2,128)}, u32[]{:S(2)}) copy-start(s32[2,13]{1,0:T(2,128)} %param.10) | copy-start | bytes 316
  159.7 71.4 %copy-start.2 = (bf16[384,448]{0,1:T(8,128)(2,1)S(1)}, bf16[384,448]{0,1:T(8,128)(2,1)}, u32[]{:S(2)}) copy-start(bf16[384,448]{0,1:T(8,128)(2,1)} %param.11) | copy-start | bytes 1032196
  226.2 120.4 %all-to-all-start.1 = ((bf16[16,256,896]{2,1,0:T(8,128)(2,1)}), bf16[16,256,896]{2,1,0:T(8,128)(2,1)}, u32[]{:S(2)}, u32[]{:S(2)}) async-start(bf16[16,256,896]{2,1,0:T(8,128)(2,1)} %pack.3), calls=%async_computation.1 | async-start | bytes 14680064 | tf_op jit(solution)/shard_map/all_to_all | solution.py:209
  231.3 126.2 %collective-permute-start.2 = (bf16[384,448]{1,0:T(8,128)(2,1)S(1)}, bf16[384,448]{1,0:T(8,128)(2,1)}, u32[]{:S(2)}, u32[]{:S(2)}) collective-permute-start(bf16[384,448]{1,0:T(8,128)(2,1)S(1)} %copy.43), channel_id=1, source_target_pairs={{0,16},{1,17},{2,18},{3,19},{4,20},{5,21},{6,22},{7,23},{8,24},{9,... | collective-permute-start | bytes 1032200 | tf_op jit(solution)/shard_map/ppermute | solution.py:224
  345.7 53.8 %collective-permute-start = (bf16[384,896]{1,0:T(8,128)(2,1)}, bf16[384,896]{1,0:T(8,128)(2,1)S(1)}, u32[]{:S(2)}, u32[]{:S(2)}) collective-permute-start(bf16[384,896]{1,0:T(8,128)(2,1)} %get-tuple-element.42), channel_id=1, source_target_pairs={{0,16},{1,17},{2,18},{3,19},{4,20},{5,21},{6,22},{7,23},{8,24},{9,... | collective-permute-start | bytes 2064392 | tf_op jit(solution)/shard_map/ppermute | solution.py:246
  355.4 58.8 %collective-permute-start.1 = (bf16[384,896]{1,0:T(8,128)(2,1)}, bf16[384,896]{1,0:T(8,128)(2,1)}, u32[]{:S(2)}, u32[]{:S(2)}) collective-permute-start(bf16[384,896]{1,0:T(8,128)(2,1)} %get-tuple-element.44), channel_id=1, source_target_pairs={{0,16},{1,17},{2,18},{3,19},{4,20},{5,21},{6,22},{7,23},{8,24},{9,... | collective-permute-start | bytes 2064392 | tf_op jit(solution)/shard_map/ppermute | solution.py:246
  399.5 14.8 %copy-start.1 = (bf16[384,896]{1,0:T(8,128)(2,1)}, bf16[384,896]{1,0:T(8,128)(2,1)S(1)}, u32[]{:S(2)}) copy-start(bf16[384,896]{1,0:T(8,128)(2,1)S(1)} %collective-permute-done) | copy-start | bytes 2064388
  497.1 51.7 %all-to-all-start.2 = ((bf16[32,256,128]{2,1,0:T(8,128)(2,1)}), bf16[32,256,128]{2,1,0:T(8,128)(2,1)S(1)}, u32[]{:S(2)}, u32[]{:S(2)}) async-start(bf16[32,256,128]{2,1,0:T(8,128)(2,1)} %bitcast.42), calls=%async_computation.2 | async-start | bytes 4194304 | tf_op jit(solution)/shard_map/all_to_all | solution.py:268
  564.9 55.1 %copy-start = (f32[16,64,64]{2,1,0:T(8,128)S(1)}, f32[16,64,64]{2,1,0:T(8,128)}, u32[]{:S(2)}) copy-start(f32[16,64,64]{2,1,0:T(8,128)} %cayley_inverse.1) | copy-start | bytes 786436
  564.9 52.9 %all-to-all-start.3 = ((bf16[32,256,128]{2,1,0:T(8,128)(2,1)}), bf16[32,256,128]{2,1,0:T(8,128)(2,1)}, u32[]{:S(2)}, u32[]{:S(2)}) async-start(bf16[32,256,128]{2,1,0:T(8,128)(2,1)} %bitcast.38), calls=%async_computation.3 | async-start | bytes 4194304 | tf_op jit(solution)/shard_map/all_to_all | solution.py:268
Sparse Core Ops, SparseCore 0:
  10.9 80.1 all-gather.5
  108.8 117.3 all-gather.3
